TPU v7x, 256 devices: a whole 4x4x8 slice. The times are simulated.
256 devices in a mesh: wide: 32 (over z_lo, y, core), narrow: 8 (over z_hi, x).
Axes of the slice: x: 4, y: 4, z: 8 (z_hi: 2, z_lo: 4; z = z_hi * 4 + z_lo), core: 2. Of those that a mesh axis runs over, the one named last changes fastest.
Arguments:
- gradient: float32 [3072, 3072], P('wide', 'narrow'), may hold values from -6 to 6
- first_moment: float32 [3072, 3072], P('wide', 'narrow'), may hold values from -6 to 6
- second_moment: float32 [3072, 3072], P('wide', 'narrow'), may hold values from 0.25 to 4
- left_basis: float32 [3072, 3072], P('wide', 'narrow'), may hold values from -0.21875 to 0.21875
- right_basis: float32 [3072, 3072], P('wide', 'narrow'), may hold values from -0.109375 to 0.109375
Outputs:
- update: float32 [3072, 3072], P('wide', 'narrow')
- new_first: float32 [3072, 3072], P('wide', 'narrow')
- new_second: float32 [3072, 3072], P('wide', 'narrow')
All inputs are finite; a program needn't handle non-finite values.
Results may differ from a plain program's by a relative error of at most 0.000075.
Values sent between devices are 32-bit elements; how exact they have to be, the bound alone decides.
No kernel may reach another device: no remote copies, remote signals or barrier semaphores. Data moves between devices by JAX's collectives and lax.ppermute only.
A program may use at most 64 MiB of HBM per device.

v0:
```python
import functools

import jax
import jax.numpy as jnp
from jax import lax
from jax.experimental import pallas as pl
from jax.experimental.pallas import tpu as pltpu
from jax.sharding import Mesh
from jax.sharding import PartitionSpec as P

STEP = 10
WIDE = ("zl", "y", "c")
NARROW = ("zh", "x")

beta_first = 0.9
beta_second = 0.95
epsilon = 1e-08

F32 = jnp.float32
BF16 = jnp.bfloat16


def shift(value, axis, by):
    n = lax.axis_size(axis)
    return lax.ppermute(value, axis, [(i, (i + by) % n) for i in range(n)])


def split(value):
    high = value.astype(BF16)
    return high, (value - high.astype(F32)).astype(BF16)


def product(left, right, dims=(1, 0)):
    def one(a, b):
        return lax.dot_general(
            a, b, (((dims[0],), (dims[1],)), ((), ())), preferred_element_type=F32
        )

    return one(left[0], right[0]) + (one(left[0], right[1]) + one(left[1], right[0]))


def call(kernel, place, arrays, outs, scratch=()):
    return pl.pallas_call(
        kernel,
        out_shape=outs,
        in_specs=[pl.BlockSpec(memory_space=pltpu.SMEM)]
        + [pl.BlockSpec(memory_space=pltpu.VMEM)] * len(arrays),
        out_specs=[pl.BlockSpec(memory_space=pltpu.VMEM)] * len(outs),
        scratch_shapes=scratch,
        compiler_params=pltpu.CompilerParams(vmem_limit_bytes=20 * 2**20),
    )(place, *arrays)


def shape(*lengths, dtype=F32):
    return jax.ShapeDtypeStruct(lengths, dtype)


ZL, Y, C, ZH, X = range(5)


def packed(value):
    rows, half = value.shape[0] // 2, value.shape[1]
    return (slice(0, half), value[:rows]), (slice(half, 2 * half), value[rows:])


def store(ref, value):
    for lanes, part in packed(value):
        ref[:, lanes] = part


def load(ref):
    half = ref.shape[1] // 2
    return split(jnp.concatenate([ref[:, :half], ref[:, half:]]))


def core_columns(tile, which):
    q = tile.shape[1] // 4
    even = jnp.concatenate([tile[:, :q], tile[:, 2 * q : 3 * q]], 1)
    odd = jnp.concatenate([tile[:, q : 2 * q], tile[:, 3 * q :]], 1)
    return jnp.where(which == 0, even, odd)


def pack_gradient_kernel(place, own, away, out):
    half = out.shape[1] // 2
    first = place[C] == 0
    mine = core_columns(own[...], place[C])
    theirs = core_columns(away[...], place[C])
    out[:, :half] = jnp.where(first, mine, theirs)
    out[:, half:] = jnp.where(first, theirs, mine)


def rotate_right_kernel(place, *refs):
    grads, rights = refs[:5], refs[5:10]
    mine, other, right, g_high, g_low = refs[10:]
    rows, cols = right.shape[1], right.shape[2]
    half = cols // 2
    first = place[C] == 0
    for dy in range(4):
        for dz in range(4):
            at = lax.rem(place[ZL] + 4 - dz, 4) * 4 + lax.rem(place[Y] + dy, 4)
            if dy == 2:
                right[at] = rights[3 + dz // 2][dz % 2]
            else:
                right[at] = rights[(0, 2, None, 1)[dy]][dz]
    for dx in range(4):
        x = lax.rem(place[X] + dx, 4)
        for r in range(2):
            at = lax.rem(place[ZH] + r, 2) * 4 + x
            if dx == 2:
                block = grads[3 + r][0]
            else:
                block = grads[(0, 2, None, 1)[dx]][r]
            tile = jnp.concatenate([block[:, :half], block[:, half:]])
            g_high[at], g_low[at] = split(tile)
    total = None
    for k in range(8):
        block = right[2 * k : 2 * k + 2].reshape(2 * rows, cols)
        term = product((g_high[k], g_low[k]), split(block))
        total = term if total is None else total + term
    store(mine, jnp.where(first, total[:, :half], total[:, half:]))
    store(other, jnp.where(first, total[:, half:], total[:, :half]))


def pack_left_kernel(place, stack, out):
    half = out.shape[-1] // 2
    for d in range(4):
        for t in range(2):
            tile = stack[2 * t + d // 2]
            lanes = slice(half * t, half * (t + 1))
            out[d, :, lanes] = tile[:, :half] if d % 2 == 0 else tile[:, half:]


def left_kernel(place, *refs):
    owns, aways = refs[:2], refs[2:4]
    high, low, t_high, t_low = refs[4:]
    rows, half = owns[0].shape[1], owns[0].shape[2] // 2
    first = place[C] == 0
    for r in range(2):
        for t in range(2):
            a = 2 * lax.rem(place[ZH] + r, 2) + t
            e = lax.rem(a + 4 - place[ZL], 4)
            for d in range(4):
                at = lax.rem(place[Y] + d, 4)
                lanes = slice(half * t, half * (t + 1))
                mine, theirs = owns[r][at, :, lanes], aways[r][at, :, lanes]
                tile = jnp.concatenate(
                    [jnp.where(first, mine, theirs), jnp.where(first, theirs, mine)]
                )
                high[e, d], low[e, d] = split(tile)
                t_high[e, d], t_low[e, d] = split(tile.T)


def rotate_left_kernel(place, *refs):
    t_high, t_low = refs[:2]
    panels, outs = refs[2:6], refs[6:]
    parts = [load(p) for p in panels]
    for e in range(4):
        total = None
        for d in range(4):
            term = product((t_high[e, d], t_low[e, d]), parts[d])
            total = term if total is None else total + term
        store(outs[e], total)


def back_left_kernel(place, *refs):
    high, low = refs[:2]
    panels, outs = refs[2:6], refs[6:]
    parts = [load(p) for p in panels]
    for d in range(4):
        total = None
        for e in range(4):
            term = product((high[e, d], low[e, d]), parts[e])
            total = term if total is None else total + term
        store(outs[d], total)


def right_kernel(place, own, away, high, low):
    rows = own.shape[1]
    for s in range(16):
        first = place[C] == 0
        mine, theirs = own[s], away[s]
        tile = jnp.concatenate(
            [jnp.where(first, mine, theirs), jnp.where(first, theirs, mine)]
        )
        at = slice(2 * rows * (s % 2), 2 * rows * (s % 2 + 1))
        high[s // 2, at], low[s // 2, at] = split(tile)


def back_right_kernel(r, place, back, high, low, *outs):
    left = split(back[...])
    zh = lax.rem(place[ZH] + r, 2)
    for f in range(4):
        k = zh * 4 + lax.rem(place[X] + f, 4)
        outs[f][...] = product(left, (high[k], low[k]), (1, 1))


def copies_sent(value, axis):
    n = lax.axis_size(axis)
    copies = jnp.broadcast_to(value[None], (n, *value.shape))
    return lax.all_to_all(copies, axis, 0, 0, tiled=True)


def ring(value, axis, tie=None):
    n = value.shape[0] // 2
    up, down = shift(value, axis, 1), shift(value, axis, -1)
    if tie is not None:
        up, down, tie = lax.optimization_barrier((up, down, tie))
    far = [shift(up[:n], axis, 1), shift(down[n:], axis, -1)]
    return [value, up, down] + far


def gathered(value, axis, by=1):
    return [value] + [shift(value, axis, by * d) for d in (1, 2, 3)]


def body(gradient, first_moment, second_moment, left_basis, right_basis):
    zl, y, c = (lax.axis_index(a) for a in WIDE)
    zh, x = (lax.axis_index(a) for a in NARROW)
    place = jnp.stack([zl, y, c, zh, x]).astype(jnp.int32)
    rows, cols = gradient.shape
    half = cols // 2
    size = 2 * rows

    def swapped(value):
        one, two = value[..., :half], value[..., half:]
        first = c == 0
        other = shift(jnp.where(first, two, one), "c", 1)
        return jnp.concatenate(
            [jnp.where(first, one, other), jnp.where(first, other, two)], -1
        )

    right_z = jnp.stack(
        [right_basis] + [shift(right_basis, "zl", d) for d in (1, 2, 3)]
    )
    (grad,) = call(
        pack_gradient_kernel,
        place,
        [gradient, shift(gradient, "c", 1)],
        [shape(rows, cols)],
    )
    grad = jnp.stack([grad, shift(grad, "zh", 1)])
    grad, right_z = lax.optimization_barrier((grad, right_z))
    left_parts = copies_sent(left_basis, "x")

    (packs,) = call(pack_left_kernel, place, [left_parts], [shape(4, rows, cols)])
    left = lax.all_to_all(packs, "y", 0, 0, tiled=True)
    left, _ = lax.optimization_barrier((left, grad))

    right_parts = ring(right_z, "y")
    grad_parts = ring(grad, "x")
    left_far = shift(left, "zh", 1)
    both = shift(jnp.stack([left, left_far]), "c", 1)
    lefts = call(
        left_kernel,
        place,
        [left, left_far, both[0], both[1]],
        [shape(4, 4, size, half, dtype=BF16)] * 2
        + [shape(4, 4, half, size, dtype=BF16)] * 2,
    )

    mine, other, right = call(
        rotate_right_kernel,
        place,
        grad_parts + right_parts,
        [shape(rows, cols)] * 2 + [shape(16, rows, cols)],
        [pltpu.VMEM((8, size, half), BF16)] * 2,
    )
    other, _ = lax.optimization_barrier((other, left_far))
    rotated_right = mine + shift(other, "c", 1)
    panels = gathered(rotated_right, "y", -1)
    terms = call(
        rotate_left_kernel, place, list(lefts[2:]) + panels, [shape(rows, cols)] * 4
    )
    rotated = terms[0] + sum(shift(terms[e], "zl", e) for e in (1, 2, 3))

    rights = call(
        right_kernel,
        place,
        [right, shift(right, "c", 1)],
        [shape(8, cols, cols, dtype=BF16)] * 2,
    )

    first, second = swapped(jnp.stack([first_moment, second_moment]))
    new_first = beta_first * first + (1.0 - beta_first) * rotated
    new_second = beta_second * second + (1.0 - beta_second) * rotated * rotated
    direction = (
        new_first
        / (1.0 - beta_first**STEP)
        / (jnp.sqrt(new_second / (1.0 - beta_second**STEP)) + epsilon)
    )
    moments = swapped(jnp.stack([new_first, new_second]))

    directions = gathered(direction, "zl", -1)
    lefts, rights = lax.optimization_barrier((lefts, rights))
    back = call(
        back_left_kernel, place, list(lefts[:2]) + directions, [shape(rows, cols)] * 4
    )
    back = swapped(back[0] + sum(shift(back[d], "y", d) for d in (1, 2, 3)))

    def summed(r):
        values = call(
            functools.partial(back_right_kernel, r),
            place,
            [back, *rights],
            [shape(rows, cols)] * 4,
        )
        return values[0] + sum(shift(values[f], "x", f) for f in (1, 2, 3))

    away = shift(summed(1), "zh", 1)
    update = summed(0) + away
    return (update, *moments)


def solution(mesh):
    torus = Mesh(mesh.devices.reshape(4, 4, 2, 2, 4), WIDE + NARROW)
    spec = P(WIDE, NARROW)
    return jax.shard_map(
        body,
        mesh=torus,
        in_specs=(spec,) * 5,
        out_specs=(spec,) * 3,
        check_vma=False,
    )
```

profile of v0, /device:TPU:33, one launch (start us, length us, event | category | flops | bytes accessed | tf_op | source)
XLA Modules:
  0.0 161.6 jit_solution(17173527802525806000)
XLA Ops:
  2.5 4.0 %all-to-all-start = ((f32[4,96,384]{2,1,0:T(8,128)}), f32[4,96,384]{2,1,0:T(8,128)S(1)}, u32[]{:S(2)}, u32[]{:S(2)}) async-start(f32[4,96,384]{2,1,0:T(8,128)} %broadcast_in_dim.2), calls=%async_computation | async-start | bytes 1179648 | tf_op jit(solution)/shard_map/all_to_all | solution.py:200
  9.1 2.8 %collective-permute-start.3 = (f32[96,384]{1,0:T(8,128)S(1)}, f32[96,384]{1,0:T(8,128)S(1)}, u32[]{:S(2)}, u32[]{:S(2)}) collective-permute-start(f32[96,384]{1,0:T(8,128)S(1)} %copy-done.12), channel_id=1, source_target_pairs={{0,128},{64,192},{128,0},{192,64},{1,129},{65,193},{129,1},{193,65... | collective-permute-start | bytes 442376 | tf_op jit(solution)/shard_map/ppermute | solution.py:25
  12.8 4.5 %collective-permute-start.1 = (f32[96,384]{1,0:T(8,128)S(1)}, f32[96,384]{1,0:T(8,128)S(1)}, u32[]{:S(2)}, u32[]{:S(2)}) collective-permute-start(f32[96,384]{1,0:T(8,128)S(1)} %shard_map.77), channel_id=1, source_target_pairs={{0,4},{4,0},{1,5},{5,1},{2,6},{6,2},{3,7},{7,3},{8,12},{12,8},{9,1... | collective-permute-start | bytes 442376 | tf_op jit(solution)/shard_map/ppermute | solution.py:25
  18.8 4.2 %all-to-all-start.1 = ((f32[4,96,384]{2,1,0:T(8,128)}), f32[4,96,384]{2,1,0:T(8,128)S(1)}, u32[]{:S(2)}, u32[]{:S(2)}) async-start(f32[4,96,384]{2,1,0:T(8,128)} %shard_map.76), calls=%async_computation.1 | async-start | bytes 1179648 | tf_op jit(solution)/shard_map/all_to_all | solution.py:246
  23.0 5.1 %collective-permute-done.3 = f32[96,384]{1,0:T(8,128)S(1)} collective-permute-done((f32[96,384]{1,0:T(8,128)S(1)}, f32[96,384]{1,0:T(8,128)S(1)}, u32[]{:S(2)}, u32[]{:S(2)}) %collective-permute-start.3) | collective-permute-done | bytes 147488 | tf_op jit(solution)/shard_map/ppermute | solution.py:25
  28.2 2.8 %collective-permute-start.12 = (f32[4,96,384]{2,1,0:T(8,128)S(1)}, f32[4,96,384]{2,1,0:T(8,128)S(1)}, u32[]{:S(2)}, u32[]{:S(2)}) collective-permute-start(f32[4,96,384]{2,1,0:T(8,128)S(1)} %pad_maximum_fusion.1.refs_5_), channel_id=1, source_target_pairs={{0,48},{16,0},{32,16},{48,32},{1,49},{17,1},{33,17},{49,33},{2,50}... | collective-permute-start | bytes 1769480 | tf_op jit(solution)/shard_map/ppermute | solution.py:25
  31.6 4.6 %collective-permute-start.5 = (f32[4,96,384]{2,1,0:T(8,128)S(1)}, f32[4,96,384]{2,1,0:T(8,128)S(1)}, u32[]{:S(2)}, u32[]{:S(2)}) collective-permute-start(f32[4,96,384]{2,1,0:T(8,128)S(1)} %all-to-all-done.1.refs_0_), channel_id=1, source_target_pairs={{0,4},{4,0},{1,5},{5,1},{2,6},{6,2},{3,7},{7,3},{8,12},{12,8},{9,1... | collective-permute-start | bytes 1769480 | tf_op jit(solution)/shard_map/ppermute | solution.py:25
  36.2 3.0 %collective-permute-start.8 = (f32[2,96,384]{2,1,0:T(8,128)S(1)}, f32[2,96,384]{2,1,0:T(8,128)S(1)}, u32[]{:S(2)}, u32[]{:S(2)}) collective-permute-start(f32[2,96,384]{2,1,0:T(8,128)S(1)} %pad_maximum_fusion.2.refs_0_), channel_id=1, source_target_pairs={{0,3},{1,0},{2,1},{3,2},{4,7},{5,4},{6,5},{7,6},{8,11},{9,8},{10,9... | collective-permute-start | bytes 884744 | tf_op jit(solution)/shard_map/ppermute | solution.py:25
  39.1 4.6 %collective-permute-done.12.refs_7_ = f32[4,96,384]{2,1,0:T(8,128)S(1)} collective-permute-done((f32[4,96,384]{2,1,0:T(8,128)S(1)}, f32[4,96,384]{2,1,0:T(8,128)S(1)}, u32[]{:S(2)}, u32[]{:S(2)}) %collective-permute-start.12) | collective-permute-done | bytes 589856 | tf_op jit(solution)/shard_map/ppermute | solution.py:25
  43.7 3.4 %collective-permute-start.14 = (f32[2,96,384]{2,1,0:T(8,128)S(1)}, f32[2,96,384]{2,1,0:T(8,128)S(1)}, u32[]{:S(2)}, u32[]{:S(2)}) collective-permute-start(f32[2,96,384]{2,1,0:T(8,128)S(1)} %slice.53), channel_id=1, source_target_pairs={{0,48},{16,0},{32,16},{48,32},{1,49},{17,1},{33,17},{49,33},{2,50}... | collective-permute-start | bytes 884744 | tf_op jit(solution)/shard_map/ppermute | solution.py:25
  47.3 3.0 %collective-permute-start.10 = (f32[1,96,384]{2,1,0:T(8,128)S(1)}, f32[1,96,384]{2,1,0:T(8,128)S(1)}, u32[]{:S(2)}, u32[]{:S(2)}) collective-permute-start(f32[1,96,384]{2,1,0:T(8,128)S(1)} %slice.51), channel_id=1, source_target_pairs={{0,3},{1,0},{2,1},{3,2},{4,7},{5,4},{6,5},{7,6},{8,11},{9,8},{10,9... | collective-permute-start | bytes 442376 | tf_op jit(solution)/shard_map/ppermute | solution.py:25
  52.4 3.7 %collective-permute-done.9.refs_3_ = f32[1,96,384]{2,1,0:T(8,128)S(1)} collective-permute-done((f32[1,96,384]{2,1,0:T(8,128)S(1)}, f32[1,96,384]{2,1,0:T(8,128)S(1)}, u32[]{:S(2)}, u32[]{:S(2)}) %collective-permute-start.9) | collective-permute-done | bytes 147488 | tf_op jit(solution)/shard_map/ppermute | solution.py:25
  60.3 3.1 %shard_map.79 = (f32[96,384]{1,0:T(8,128)S(1)}, f32[96,384]{1,0:T(8,128)}, f32[16,96,384]{2,1,0:T(8,128)S(1)}) custom-call(s32[5]{0:T(128)S(1)} %stack.74.place, f32[2,96,384]{2,1,0:T(8,128)S(1)} %copy-done.7, f32[2,96,384]{2,1,0:T(8,128)S(1)} %collective-permute-done.7.refs_1_, f32[2,96,384]{2,1,0:T(8,128)S(1)} %collective-permute-done.8.refs_2_, ...), custom_call_target="tpu_custom_call" | custom-call | tf_op jit(solution)/shard_map/pallas_call | solution.py:43
  64.1 2.8 %collective-permute-start.15 = (f32[16,96,384]{2,1,0:T(8,128)S(1)}, f32[16,96,384]{2,1,0:T(8,128)}, u32[]{:S(2)}, u32[]{:S(2)}) collective-permute-start(f32[16,96,384]{2,1,0:T(8,128)S(1)} %get-tuple-element.43.own), channel_id=1, source_target_pairs={{0,8},{8,0},{1,9},{9,1},{2,10},{10,2},{3,11},{11,3},{4,12},{12,4},... | collective-permute-start | bytes 7077896 | tf_op jit(solution)/shard_map/ppermute | solution.py:25
  69.7 3.8 %collective-permute-done.17 = f32[96,384]{1,0:T(8,128)} collective-permute-done((f32[96,384]{1,0:T(8,128)}, f32[96,384]{1,0:T(8,128)}, u32[]{:S(2)}, u32[]{:S(2)}) %collective-permute-start.17) | collective-permute-done | bytes 147488 | tf_op jit(solution)/shard_map/ppermute | solution.py:25
  74.9 3.9 %collective-permute-start.19 = (f32[96,384]{1,0:T(8,128)S(1)}, f32[96,384]{1,0:T(8,128)S(1)}, u32[]{:S(2)}, u32[]{:S(2)}) collective-permute-start(f32[96,384]{1,0:T(8,128)S(1)} %add.54.refs_2_), channel_id=1, source_target_pairs={{0,32},{16,48},{32,0},{48,16},{1,33},{17,49},{33,1},{49,17},{2,34}... | collective-permute-start | bytes 442376 | tf_op jit(solution)/shard_map/ppermute | solution.py:25
  80.1 2.5 %shard_map.78 = (bf16[4,4,192,192]{3,2,1,0:T(8,128)(2,1)S(1)}, bf16[4,4,192,192]{3,2,1,0:T(8,128)(2,1)S(1)}, bf16[4,4,192,192]{3,2,1,0:T(8,128)(2,1)S(1)}, bf16[4,4,192,192]{3,2,1,0:T(8,128)(2,1)S(1)}) custom-call(s32[5]{0:T(128)S(1)} %stack.74.place, f32[4,96,384]{2,1,0:T(8,128)S(1)} %all-to-all-done.1.refs_0_, ...), custom_call_target="tpu_custom_call" | custom-call | tf_op jit(solution)/shard_map/pallas_call | solution.py:43
  82.6 2.9 %collective-permute-done.19.refs_4_ = f32[96,384]{1,0:T(8,128)S(1)} collective-permute-done((f32[96,384]{1,0:T(8,128)S(1)}, f32[96,384]{1,0:T(8,128)S(1)}, u32[]{:S(2)}, u32[]{:S(2)}) %collective-permute-start.19) | collective-permute-done | bytes 147488 | tf_op jit(solution)/shard_map/ppermute | solution.py:25
  85.5 2.1 %shard_map.81 = (f32[96,384]{1,0:T(8,128)S(1)}, f32[96,384]{1,0:T(8,128)S(1)}, f32[96,384]{1,0:T(8,128)S(1)}, f32[96,384]{1,0:T(8,128)S(1)}) custom-call(s32[5]{0:T(128)S(1)} %stack.74.place, bf16[4,4,192,192]{3,2,1,0:T(8,128)(2,1)S(1)} %get-tuple-element.40.refs_0_, bf16[4,4,192,192]{3,2,1,0:T(8,128)(2,1)S(1)} %get-tuple-element.41.refs_1_, ...), custom_call_target="tpu_custom_call" | custom-call | tf_op jit(solution)/shard_map/pallas_call | solution.py:43
  87.6 2.4 %collective-permute-start.21 = (f32[96,384]{1,0:T(8,128)S(1)}, f32[96,384]{1,0:T(8,128)S(1)}, u32[]{:S(2)}, u32[]{:S(2)}) collective-permute-start(f32[96,384]{1,0:T(8,128)S(1)} %get-tuple-element.52), channel_id=1, source_target_pairs={{0,64},{64,128},{128,192},{192,0},{1,65},{65,129},{129,193},{193,1... | collective-permute-start | bytes 442376 | tf_op jit(solution)/shard_map/ppermute | solution.py:25
  90.0 3.0 %collective-permute-start.22 = (f32[96,384]{1,0:T(8,128)S(1)}, f32[96,384]{1,0:T(8,128)S(1)}, u32[]{:S(2)}, u32[]{:S(2)}) collective-permute-start(f32[96,384]{1,0:T(8,128)S(1)} %get-tuple-element.53), channel_id=1, source_target_pairs={{0,128},{64,192},{128,0},{192,64},{1,129},{65,193},{129,1},{193,65... | collective-permute-start | bytes 442376 | tf_op jit(solution)/shard_map/ppermute | solution.py:25
  93.9 8.7 %collective-permute-done.22 = f32[96,384]{1,0:T(8,128)S(1)} collective-permute-done((f32[96,384]{1,0:T(8,128)S(1)}, f32[96,384]{1,0:T(8,128)S(1)}, u32[]{:S(2)}, u32[]{:S(2)}) %collective-permute-start.22) | collective-permute-done | bytes 147488 | tf_op jit(solution)/shard_map/ppermute | solution.py:25
  102.5 2.7 %collective-permute-done.23 = f32[96,384]{1,0:T(8,128)S(1)} collective-permute-done((f32[96,384]{1,0:T(8,128)S(1)}, f32[96,384]{1,0:T(8,128)S(1)}, u32[]{:S(2)}, u32[]{:S(2)}) %collective-permute-start.23) | collective-permute-done | bytes 147488 | tf_op jit(solution)/shard_map/ppermute | solution.py:25
  107.7 2.8 %shard_map.80 = (bf16[8,384,384]{2,1,0:T(8,128)(2,1)S(1)}, bf16[8,384,384]{2,1,0:T(8,128)(2,1)S(1)}) custom-call(s32[5]{0:T(128)S(1)} %stack.74.place, f32[16,96,384]{2,1,0:T(8,128)S(1)} %get-tuple-element.43.own, f32[16,96,384]{2,1,0:T(8,128)} %collective-permute-done.15.away), custom_call_target="tpu_custom_call" | custom-call | tf_op jit(solution)/shard_map/pallas_call | solution.py:43
  110.5 6.8 %collective-permute-done.25.refs_4_ = f32[96,384]{1,0:T(8,128)S(1)} collective-permute-done((f32[96,384]{1,0:T(8,128)S(1)}, f32[96,384]{1,0:T(8,128)S(1)}, u32[]{:S(2)}, u32[]{:S(2)}) %collective-permute-start.25) | collective-permute-done | bytes 147488 | tf_op jit(solution)/shard_map/ppermute | solution.py:25
  117.3 3.2 %collective-permute-done.24.refs_3_ = f32[96,384]{1,0:T(8,128)S(1)} collective-permute-done((f32[96,384]{1,0:T(8,128)S(1)}, f32[96,384]{1,0:T(8,128)S(1)}, u32[]{:S(2)}, u32[]{:S(2)}) %collective-permute-start.24) | collective-permute-done | bytes 147488 | tf_op jit(solution)/shard_map/ppermute | solution.py:25
  120.5 2.1 %shard_map.82 = (f32[96,384]{1,0:T(8,128)S(1)}, f32[96,384]{1,0:T(8,128)S(1)}, f32[96,384]{1,0:T(8,128)S(1)}, f32[96,384]{1,0:T(8,128)S(1)}) custom-call(s32[5]{0:T(128)S(1)} %stack.74.place, bf16[4,4,192,192]{3,2,1,0:T(8,128)(2,1)S(1)} %get-tuple-element.46.refs_0_, bf16[4,4,192,192]{3,2,1,0:T(8,128)(2,1)S(1)} %get-tuple-element.47.refs_1_, ...), custom_call_target="tpu_custom_call" | custom-call | tf_op jit(solution)/shard_map/pallas_call | solution.py:43
  123.1 3.4 %collective-permute-start.28 = (f32[96,384]{1,0:T(8,128)S(1)}, f32[96,384]{1,0:T(8,128)S(1)}, u32[]{:S(2)}, u32[]{:S(2)}) collective-permute-start(f32[96,384]{1,0:T(8,128)S(1)} %get-tuple-element.57), channel_id=1, source_target_pairs={{0,32},{16,48},{32,0},{48,16},{1,33},{17,49},{33,1},{49,17},{2,34}... | collective-permute-start | bytes 442376 | tf_op jit(solution)/shard_map/ppermute | solution.py:25
  126.5 2.3 %collective-permute-done.27 = f32[96,384]{1,0:T(8,128)S(1)} collective-permute-done((f32[96,384]{1,0:T(8,128)S(1)}, f32[96,384]{1,0:T(8,128)S(1)}, u32[]{:S(2)}, u32[]{:S(2)}) %collective-permute-start.27) | collective-permute-done | bytes 147488 | tf_op jit(solution)/shard_map/ppermute | solution.py:25
  128.8 4.3 %collective-permute-done.28 = f32[96,384]{1,0:T(8,128)S(1)} collective-permute-done((f32[96,384]{1,0:T(8,128)S(1)}, f32[96,384]{1,0:T(8,128)S(1)}, u32[]{:S(2)}, u32[]{:S(2)}) %collective-permute-start.28) | collective-permute-done | bytes 147488 | tf_op jit(solution)/shard_map/ppermute | solution.py:25
  148.2 4.6 %collective-permute-start.37 = (f32[96,384]{1,0:T(8,128)S(1)}, f32[96,384]{1,0:T(8,128)S(1)}, u32[]{:S(2)}, u32[]{:S(2)}) collective-permute-start(f32[96,384]{1,0:T(8,128)S(1)} %add_add_fusion), channel_id=1, source_target_pairs={{0,4},{4,0},{1,5},{5,1},{2,6},{6,2},{3,7},{7,3},{8,12},{12,8},{9,1... | collective-permute-start | bytes 442376 | tf_op jit(solution)/shard_map/ppermute | solution.py:25
  153.8 7.1 %collective-permute-done.37 = f32[96,384]{1,0:T(8,128)S(1)} collective-permute-done((f32[96,384]{1,0:T(8,128)S(1)}, f32[96,384]{1,0:T(8,128)S(1)}, u32[]{:S(2)}, u32[]{:S(2)}) %collective-permute-start.37) | collective-permute-done | bytes 147488 | tf_op jit(solution)/shard_map/ppermute | solution.py:25
  (109 shorter events, 40.6 us)
Async XLA Ops:
  2.5 14.8 %all-to-all-start = ((f32[4,96,384]{2,1,0:T(8,128)}), f32[4,96,384]{2,1,0:T(8,128)S(1)}, u32[]{:S(2)}, u32[]{:S(2)}) async-start(f32[4,96,384]{2,1,0:T(8,128)} %broadcast_in_dim.2), calls=%async_computation | async-start | bytes 1179648 | tf_op jit(solution)/shard_map/all_to_all | solution.py:200
  7.5 15.5 %collective-permute-start.2 = (f32[96,384]{1,0:T(8,128)S(1)}, f32[96,384]{1,0:T(8,128)S(1)}, u32[]{:S(2)}, u32[]{:S(2)}) collective-permute-start(f32[96,384]{1,0:T(8,128)S(1)} %copy-done.12), channel_id=1, source_target_pairs={{0,64},{64,128},{128,192},{192,0},{1,65},{65,129},{129,193},{193,1... | collective-permute-start | bytes 442376 | tf_op jit(solution)/shard_map/ppermute | solution.py:25
  9.1 13.9 %collective-permute-start.4 = (f32[96,384]{1,0:T(8,128)S(1)}, f32[96,384]{1,0:T(8,128)S(1)}, u32[]{:S(2)}, u32[]{:S(2)}) collective-permute-start(f32[96,384]{1,0:T(8,128)S(1)} %copy-done.12), channel_id=1, source_target_pairs={{0,192},{64,0},{128,64},{192,128},{1,193},{65,1},{129,65},{193,129... | collective-permute-start | bytes 442376 | tf_op jit(solution)/shard_map/ppermute | solution.py:25
  9.1 19.0 %collective-permute-start.3 = (f32[96,384]{1,0:T(8,128)S(1)}, f32[96,384]{1,0:T(8,128)S(1)}, u32[]{:S(2)}, u32[]{:S(2)}) collective-permute-start(f32[96,384]{1,0:T(8,128)S(1)} %copy-done.12), channel_id=1, source_target_pairs={{0,128},{64,192},{128,0},{192,64},{1,129},{65,193},{129,1},{193,65... | collective-permute-start | bytes 442376 | tf_op jit(solution)/shard_map/ppermute | solution.py:25
  12.8 15.4 %collective-permute-start.1 = (f32[96,384]{1,0:T(8,128)S(1)}, f32[96,384]{1,0:T(8,128)S(1)}, u32[]{:S(2)}, u32[]{:S(2)}) collective-permute-start(f32[96,384]{1,0:T(8,128)S(1)} %shard_map.77), channel_id=1, source_target_pairs={{0,4},{4,0},{1,5},{5,1},{2,6},{6,2},{3,7},{7,3},{8,12},{12,8},{9,1... | collective-permute-start | bytes 442376 | tf_op jit(solution)/shard_map/ppermute | solution.py:25
  18.8 12.8 %all-to-all-start.1 = ((f32[4,96,384]{2,1,0:T(8,128)}), f32[4,96,384]{2,1,0:T(8,128)S(1)}, u32[]{:S(2)}, u32[]{:S(2)}) async-start(f32[4,96,384]{2,1,0:T(8,128)} %shard_map.76), calls=%async_computation.1 | async-start | bytes 1179648 | tf_op jit(solution)/shard_map/all_to_all | solution.py:246
  28.2 15.5 %collective-permute-start.12 = (f32[4,96,384]{2,1,0:T(8,128)S(1)}, f32[4,96,384]{2,1,0:T(8,128)S(1)}, u32[]{:S(2)}, u32[]{:S(2)}) collective-permute-start(f32[4,96,384]{2,1,0:T(8,128)S(1)} %pad_maximum_fusion.1.refs_5_), channel_id=1, source_target_pairs={{0,48},{16,0},{32,16},{48,32},{1,49},{17,1},{33,17},{49,33},{2,50}... | collective-permute-start | bytes 1769480 | tf_op jit(solution)/shard_map/ppermute | solution.py:25
  31.0 16.1 %collective-permute-start.11 = (f32[4,96,384]{2,1,0:T(8,128)S(1)}, f32[4,96,384]{2,1,0:T(8,128)S(1)}, u32[]{:S(2)}, u32[]{:S(2)}) collective-permute-start(f32[4,96,384]{2,1,0:T(8,128)S(1)} %pad_maximum_fusion.1.refs_5_), channel_id=1, source_target_pairs={{0,16},{16,32},{32,48},{48,0},{1,17},{17,33},{33,49},{49,1},{2,18}... | collective-permute-start | bytes 1769480 | tf_op jit(solution)/shard_map/ppermute | solution.py:25
  31.6 35.3 %collective-permute-start.5 = (f32[4,96,384]{2,1,0:T(8,128)S(1)}, f32[4,96,384]{2,1,0:T(8,128)S(1)}, u32[]{:S(2)}, u32[]{:S(2)}) collective-permute-start(f32[4,96,384]{2,1,0:T(8,128)S(1)} %all-to-all-done.1.refs_0_), channel_id=1, source_target_pairs={{0,4},{4,0},{1,5},{5,1},{2,6},{6,2},{3,7},{7,3},{8,12},{12,8},{9,1... | collective-permute-start | bytes 1769480 | tf_op jit(solution)/shard_map/ppermute | solution.py:25
  36.2 11.1 %collective-permute-start.8 = (f32[2,96,384]{2,1,0:T(8,128)S(1)}, f32[2,96,384]{2,1,0:T(8,128)S(1)}, u32[]{:S(2)}, u32[]{:S(2)}) collective-permute-start(f32[2,96,384]{2,1,0:T(8,128)S(1)} %pad_maximum_fusion.2.refs_0_), channel_id=1, source_target_pairs={{0,3},{1,0},{2,1},{3,2},{4,7},{5,4},{6,5},{7,6},{8,11},{9,8},{10,9... | collective-permute-start | bytes 884744 | tf_op jit(solution)/shard_map/ppermute | solution.py:25
  39.1 11.2 %collective-permute-start.7 = (f32[2,96,384]{2,1,0:T(8,128)S(1)}, f32[2,96,384]{2,1,0:T(8,128)S(1)}, u32[]{:S(2)}, u32[]{:S(2)}) collective-permute-start(f32[2,96,384]{2,1,0:T(8,128)S(1)} %pad_maximum_fusion.2.refs_0_), channel_id=1, source_target_pairs={{0,1},{1,2},{2,3},{3,0},{4,5},{5,6},{6,7},{7,4},{8,9},{9,10},{10,1... | collective-permute-start | bytes 884744 | tf_op jit(solution)/shard_map/ppermute | solution.py:25
  43.7 12.4 %collective-permute-start.14 = (f32[2,96,384]{2,1,0:T(8,128)S(1)}, f32[2,96,384]{2,1,0:T(8,128)S(1)}, u32[]{:S(2)}, u32[]{:S(2)}) collective-permute-start(f32[2,96,384]{2,1,0:T(8,128)S(1)} %slice.53), channel_id=1, source_target_pairs={{0,48},{16,0},{32,16},{48,32},{1,49},{17,1},{33,17},{49,33},{2,50}... | collective-permute-start | bytes 884744 | tf_op jit(solution)/shard_map/ppermute | solution.py:25
  47.2 9.0 %collective-permute-start.13 = (f32[2,96,384]{2,1,0:T(8,128)S(1)}, f32[2,96,384]{2,1,0:T(8,128)S(1)}, u32[]{:S(2)}, u32[]{:S(2)}) collective-permute-start(f32[2,96,384]{2,1,0:T(8,128)S(1)} %slice.52), channel_id=1, source_target_pairs={{0,16},{16,32},{32,48},{48,0},{1,17},{17,33},{33,49},{49,1},{2,18}... | collective-permute-start | bytes 884744 | tf_op jit(solution)/shard_map/ppermute | solution.py:25
  64.1 43.6 %collective-permute-start.15 = (f32[16,96,384]{2,1,0:T(8,128)S(1)}, f32[16,96,384]{2,1,0:T(8,128)}, u32[]{:S(2)}, u32[]{:S(2)}) collective-permute-start(f32[16,96,384]{2,1,0:T(8,128)S(1)} %get-tuple-element.43.own), channel_id=1, source_target_pairs={{0,8},{8,0},{1,9},{9,1},{2,10},{10,2},{3,11},{11,3},{4,12},{12,4},... | collective-permute-start | bytes 7077896 | tf_op jit(solution)/shard_map/ppermute | solution.py:25
  67.9 10.8 %collective-permute-start.6 = (f32[2,4,96,384]{3,2,1,0:T(8,128)}, f32[2,4,96,384]{3,2,1,0:T(8,128)}, u32[]{:S(2)}, u32[]{:S(2)}) collective-permute-start(f32[2,4,96,384]{3,2,1,0:T(8,128)} %pad_maximum_fusion), channel_id=1, source_target_pairs={{0,8},{8,0},{1,9},{9,1},{2,10},{10,2},{3,11},{11,3},{4,12},{12,4},... | collective-permute-start | bytes 3538952 | tf_op jit(solution)/shard_map/ppermute | solution.py:25
  69.6 23.8 %collective-permute-start.16 = (f32[2,96,192]{2,1,0:T(8,128)S(1)}, f32[2,96,192]{2,1,0:T(8,128)S(1)}, u32[]{:S(2)}, u32[]{:S(2)}) collective-permute-start(f32[2,96,192]{2,1,0:T(8,128)S(1)} %fusion.12), channel_id=1, source_target_pairs={{0,8},{8,0},{1,9},{9,1},{2,10},{10,2},{3,11},{11,3},{4,12},{12,4},... | collective-permute-start | bytes 442376 | tf_op jit(solution)/shard_map/ppermute | solution.py:25
  74.5 8.0 %collective-permute-start.20 = (f32[96,384]{1,0:T(8,128)S(1)}, f32[96,384]{1,0:T(8,128)S(1)}, u32[]{:S(2)}, u32[]{:S(2)}) collective-permute-start(f32[96,384]{1,0:T(8,128)S(1)} %add.54.refs_2_), channel_id=1, source_target_pairs={{0,16},{16,32},{32,48},{48,0},{1,17},{17,33},{33,49},{49,1},{2,18}... | collective-permute-start | bytes 442376 | tf_op jit(solution)/shard_map/ppermute | solution.py:25
  74.9 10.6 %collective-permute-start.19 = (f32[96,384]{1,0:T(8,128)S(1)}, f32[96,384]{1,0:T(8,128)S(1)}, u32[]{:S(2)}, u32[]{:S(2)}) collective-permute-start(f32[96,384]{1,0:T(8,128)S(1)} %add.54.refs_2_), channel_id=1, source_target_pairs={{0,32},{16,48},{32,0},{48,16},{1,33},{17,49},{33,1},{49,17},{2,34}... | collective-permute-start | bytes 442376 | tf_op jit(solution)/shard_map/ppermute | solution.py:25
  78.7 6.8 %collective-permute-start.18 = (f32[96,384]{1,0:T(8,128)S(1)}, f32[96,384]{1,0:T(8,128)S(1)}, u32[]{:S(2)}, u32[]{:S(2)}) collective-permute-start(f32[96,384]{1,0:T(8,128)S(1)} %add.54.refs_2_), channel_id=1, source_target_pairs={{0,48},{16,0},{32,16},{48,32},{1,49},{17,1},{33,17},{49,33},{2,50}... | collective-permute-start | bytes 442376 | tf_op jit(solution)/shard_map/ppermute | solution.py:25
  90.0 12.5 %collective-permute-start.22 = (f32[96,384]{1,0:T(8,128)S(1)}, f32[96,384]{1,0:T(8,128)S(1)}, u32[]{:S(2)}, u32[]{:S(2)}) collective-permute-start(f32[96,384]{1,0:T(8,128)S(1)} %get-tuple-element.53), channel_id=1, source_target_pairs={{0,128},{64,192},{128,0},{192,64},{1,129},{65,193},{129,1},{193,65... | collective-permute-start | bytes 442376 | tf_op jit(solution)/shard_map/ppermute | solution.py:25
  93.0 12.2 %collective-permute-start.23 = (f32[96,384]{1,0:T(8,128)S(1)}, f32[96,384]{1,0:T(8,128)S(1)}, u32[]{:S(2)}, u32[]{:S(2)}) collective-permute-start(f32[96,384]{1,0:T(8,128)S(1)} %get-tuple-element.54), channel_id=1, source_target_pairs={{0,192},{64,0},{128,64},{192,128},{1,193},{65,1},{129,65},{193,129... | collective-permute-start | bytes 442376 | tf_op jit(solution)/shard_map/ppermute | solution.py:25
  105.8 11.5 %collective-permute-start.25 = (f32[96,384]{1,0:T(8,128)S(1)}, f32[96,384]{1,0:T(8,128)S(1)}, u32[]{:S(2)}, u32[]{:S(2)}) collective-permute-start(f32[96,384]{1,0:T(8,128)S(1)} %get-tuple-element.71.refs_2_), channel_id=1, source_target_pairs={{0,128},{64,192},{128,0},{192,64},{1,129},{65,193},{129,1},{193,65... | collective-permute-start | bytes 442376 | tf_op jit(solution)/shard_map/ppermute | solution.py:25
  106.3 14.2 %collective-permute-start.24 = (f32[96,384]{1,0:T(8,128)S(1)}, f32[96,384]{1,0:T(8,128)S(1)}, u32[]{:S(2)}, u32[]{:S(2)}) collective-permute-start(f32[96,384]{1,0:T(8,128)S(1)} %get-tuple-element.71.refs_2_), channel_id=1, source_target_pairs={{0,192},{64,0},{128,64},{192,128},{1,193},{65,1},{129,65},{193,129... | collective-permute-start | bytes 442376 | tf_op jit(solution)/shard_map/ppermute | solution.py:25
  123.1 10.0 %collective-permute-start.28 = (f32[96,384]{1,0:T(8,128)S(1)}, f32[96,384]{1,0:T(8,128)S(1)}, u32[]{:S(2)}, u32[]{:S(2)}) collective-permute-start(f32[96,384]{1,0:T(8,128)S(1)} %get-tuple-element.57), channel_id=1, source_target_pairs={{0,32},{16,48},{32,0},{48,16},{1,33},{17,49},{33,1},{49,17},{2,34}... | collective-permute-start | bytes 442376 | tf_op jit(solution)/shard_map/ppermute | solution.py:25
  137.7 7.2 %collective-permute-start.34 = (f32[96,384]{1,0:T(8,128)S(1)}, f32[96,384]{1,0:T(8,128)S(1)}, u32[]{:S(2)}, u32[]{:S(2)}) collective-permute-start(f32[96,384]{1,0:T(8,128)S(1)} %get-tuple-element.66), channel_id=1, source_target_pairs={{0,1},{1,2},{2,3},{3,0},{4,5},{5,6},{6,7},{7,4},{8,9},{9,10},{10,1... | collective-permute-start | bytes 442376 | tf_op jit(solution)/shard_map/ppermute | solution.py:25
  137.8 8.6 %collective-permute-start.35 = (f32[96,384]{1,0:T(8,128)S(1)}, f32[96,384]{1,0:T(8,128)S(1)}, u32[]{:S(2)}, u32[]{:S(2)}) collective-permute-start(f32[96,384]{1,0:T(8,128)S(1)} %get-tuple-element.67), channel_id=1, source_target_pairs={{0,2},{1,3},{2,0},{3,1},{4,6},{5,7},{6,4},{7,5},{8,10},{9,11},{10,... | collective-permute-start | bytes 442376 | tf_op jit(solution)/shard_map/ppermute | solution.py:25
  139.6 8.6 %collective-permute-start.36 = (f32[96,384]{1,0:T(8,128)S(1)}, f32[96,384]{1,0:T(8,128)S(1)}, u32[]{:S(2)}, u32[]{:S(2)}) collective-permute-start(f32[96,384]{1,0:T(8,128)S(1)} %get-tuple-element.68), channel_id=1, source_target_pairs={{0,3},{1,0},{2,1},{3,2},{4,7},{5,4},{6,5},{7,6},{8,11},{9,8},{10,9... | collective-permute-start | bytes 442376 | tf_op jit(solution)/shard_map/ppermute | solution.py:25
  140.9 11.9 %collective-permute-start.38 = (f32[2,96,192]{2,1,0:T(8,128)S(1)}, f32[2,96,192]{2,1,0:T(8,128)S(1)}, u32[]{:S(2)}, u32[]{:S(2)}) collective-permute-start(f32[2,96,192]{2,1,0:T(8,128)S(1)} %fusion.14), channel_id=1, source_target_pairs={{0,8},{8,0},{1,9},{9,1},{2,10},{10,2},{3,11},{11,3},{4,12},{12,4},... | collective-permute-start | bytes 442376 | tf_op jit(solution)/shard_map/ppermute | solution.py:25
  144.0 9.8 %collective-permute-start.31 = (f32[96,384]{1,0:T(8,128)S(1)}, f32[96,384]{1,0:T(8,128)S(1)}, u32[]{:S(2)}, u32[]{:S(2)}) collective-permute-start(f32[96,384]{1,0:T(8,128)S(1)} %get-tuple-element.62), channel_id=1, source_target_pairs={{0,1},{1,2},{2,3},{3,0},{4,5},{5,6},{6,7},{7,4},{8,9},{9,10},{10,1... | collective-permute-start | bytes 442376 | tf_op jit(solution)/shard_map/ppermute | solution.py:25
  144.9 8.9 %collective-permute-start.32 = (f32[96,384]{1,0:T(8,128)S(1)}, f32[96,384]{1,0:T(8,128)S(1)}, u32[]{:S(2)}, u32[]{:S(2)}) collective-permute-start(f32[96,384]{1,0:T(8,128)S(1)} %get-tuple-element.63), channel_id=1, source_target_pairs={{0,2},{1,3},{2,0},{3,1},{4,6},{5,7},{6,4},{7,5},{8,10},{9,11},{10,... | collective-permute-start | bytes 442376 | tf_op jit(solution)/shard_map/ppermute | solution.py:25
  146.4 7.4 %collective-permute-start.33 = (f32[96,384]{1,0:T(8,128)S(1)}, f32[96,384]{1,0:T(8,128)S(1)}, u32[]{:S(2)}, u32[]{:S(2)}) collective-permute-start(f32[96,384]{1,0:T(8,128)S(1)} %get-tuple-element.64), channel_id=1, source_target_pairs={{0,3},{1,0},{2,1},{3,2},{4,7},{5,4},{6,5},{7,6},{8,11},{9,8},{10,9... | collective-permute-start | bytes 442376 | tf_op jit(solution)/shard_map/ppermute | solution.py:25
  148.2 12.6 %collective-permute-start.37 = (f32[96,384]{1,0:T(8,128)S(1)}, f32[96,384]{1,0:T(8,128)S(1)}, u32[]{:S(2)}, u32[]{:S(2)}) collective-permute-start(f32[96,384]{1,0:T(8,128)S(1)} %add_add_fusion), channel_id=1, source_target_pairs={{0,4},{4,0},{1,5},{5,1},{2,6},{6,2},{3,7},{7,3},{8,12},{12,8},{9,1... | collective-permute-start | bytes 442376 | tf_op jit(solution)/shard_map/ppermute | solution.py:25
  (22 other events, 159.2 us)
where the time goes:
time: 162 us
  starting transfers between devices  68.7 us (42%)
  waiting for transfers between devices  59.4 us (37%)
  Pallas kernels  18.5 us (11%)
  local copies, waits for them, and re-layouts  8.14 us (5%)
  other arithmetic  5.78 us (4%)
    ppermute x39, starting transfers between devices, shift(): return lax.ppermute(value, axis, [(i, (i + by) % n) for i in range(n)])  60.5 us
    ppermute x39, waiting for transfers between devices, shift(): return lax.ppermute(value, axis, [(i, (i + by) % n) for i in range(n)])  58.9 us
    pallas_call x9, Pallas kernels, call(): pl.pallas_call(kernel, out_shape=outs, in_specs=[pl.BlockSpec(memory_spac...  18.5 us
    unnamed x26, local copies, waits for them, and re-layouts  4.84 us
    all_to_all x1, starting transfers between devices, body(): left = lax.all_to_all(packs, 'y', 0, 0, tiled=True)  4.18 us
    all_to_all x1, starting transfers between devices, copies_sent(): return lax.all_to_all(copies, axis, 0, 0, tiled=True)  4.01 us
  transfers between devices with their start and end apart: 41, of which 18 were waited for; matrix products, arithmetic and copies ran while one was open for 4% of the time, Pallas kernels for 9%

commit v1 on v0

--- a/solution.py
+++ b/solution.py
@@ -249,6 +249,17 @@
     right_parts = ring(right_z, "y")
     grad_parts = ring(grad, "x")
     left_far = shift(left, "zh", 1)
+    mine, other, right = call(
+        rotate_right_kernel,
+        place,
+        grad_parts + right_parts,
+        [shape(rows, cols)] * 2 + [shape(16, rows, cols)],
+        [pltpu.VMEM((8, size, half), BF16)] * 2,
+    )
+    other, _ = lax.optimization_barrier((other, left_far))
+    other = shift(other, "c", 1)
+    left_far, other = lax.optimization_barrier((left_far, other))
+    rotated_right = mine + other
     both = shift(jnp.stack([left, left_far]), "c", 1)
     lefts = call(
         left_kernel,
@@ -258,15 +269,6 @@
         + [shape(4, 4, half, size, dtype=BF16)] * 2,
     )
 
-    mine, other, right = call(
-        rotate_right_kernel,
-        place,
-        grad_parts + right_parts,
-        [shape(rows, cols)] * 2 + [shape(16, rows, cols)],
-        [pltpu.VMEM((8, size, half), BF16)] * 2,
-    )
-    other, _ = lax.optimization_barrier((other, left_far))
-    rotated_right = mine + shift(other, "c", 1)
     panels = gathered(rotated_right, "y", -1)
     terms = call(
         rotate_left_kernel, place, list(lefts[2:]) + panels, [shape(rows, cols)] * 4

time: 162 us -> 160 us (0.988)
  waiting for transfers between devices: 59.4 us -> 56.5 us
    ppermute x39, waiting for transfers between devices: 58.9 us -> 55.9 us  [shift(): return lax.ppermute(value, axis, [(i, (i + by) % n) for i in range(n)])]
    unnamed x26 -> x28, local copies, waits for them, and re-layouts: 4.84 us -> 5.49 us
where the time goes in v1:
time: 160 us; the launch traced here: 159 us
  starting transfers between devices  68.9 us (43%)
  waiting for transfers between devices  56.5 us (35%)
  Pallas kernels  17.9 us (11%)
  local copies, waits for them, and re-layouts  8.81 us (6%)
  other arithmetic  5.78 us (4%)
    ppermute x39, starting transfers between devices, shift(): return lax.ppermute(value, axis, [(i, (i + by) % n) for i in range(n)])  60.7 us
    ppermute x39, waiting for transfers between devices, shift(): return lax.ppermute(value, axis, [(i, (i + by) % n) for i in range(n)])  55.9 us
    pallas_call x9, Pallas kernels, call(): pl.pallas_call(kernel, out_shape=outs, in_specs=[pl.BlockSpec(memory_spac...  17.9 us
    unnamed x28, local copies, waits for them, and re-layouts  5.49 us
    all_to_all x1, starting transfers between devices, body(): left = lax.all_to_all(packs, 'y', 0, 0, tiled=True)  4.18 us
    all_to_all x1, starting transfers between devices, copies_sent(): return lax.all_to_all(copies, axis, 0, 0, tiled=True)  4.01 us
  transfers between devices with their start and end apart: 41, of which 18 were waited for; matrix products, arithmetic and copies ran while one was open for 4% of the time, Pallas kernels for 9%

profile of v1, /device:TPU:33, one launch (start us, length us, event | category | flops | bytes accessed | tf_op | source)
XLA Modules:
  0.0 158.8 jit_solution(16724688084436297809)
XLA Ops:
  2.5 4.0 %all-to-all-start = ((f32[4,96,384]{2,1,0:T(8,128)}), f32[4,96,384]{2,1,0:T(8,128)S(1)}, u32[]{:S(2)}, u32[]{:S(2)}) async-start(f32[4,96,384]{2,1,0:T(8,128)} %broadcast_in_dim.2), calls=%async_computation | async-start | bytes 1179648 | tf_op jit(solution)/shard_map/all_to_all | solution.py:200
  9.1 2.8 %collective-permute-start.3 = (f32[96,384]{1,0:T(8,128)S(1)}, f32[96,384]{1,0:T(8,128)S(1)}, u32[]{:S(2)}, u32[]{:S(2)}) collective-permute-start(f32[96,384]{1,0:T(8,128)S(1)} %copy-done.12), channel_id=1, source_target_pairs={{0,128},{64,192},{128,0},{192,64},{1,129},{65,193},{129,1},{193,65... | collective-permute-start | bytes 442376 | tf_op jit(solution)/shard_map/ppermute | solution.py:25
  12.8 4.5 %collective-permute-start.1 = (f32[96,384]{1,0:T(8,128)S(1)}, f32[96,384]{1,0:T(8,128)S(1)}, u32[]{:S(2)}, u32[]{:S(2)}) collective-permute-start(f32[96,384]{1,0:T(8,128)S(1)} %shard_map.77), channel_id=1, source_target_pairs={{0,4},{4,0},{1,5},{5,1},{2,6},{6,2},{3,7},{7,3},{8,12},{12,8},{9,1... | collective-permute-start | bytes 442376 | tf_op jit(solution)/shard_map/ppermute | solution.py:25
  18.8 4.2 %all-to-all-start.1 = ((f32[4,96,384]{2,1,0:T(8,128)}), f32[4,96,384]{2,1,0:T(8,128)S(1)}, u32[]{:S(2)}, u32[]{:S(2)}) async-start(f32[4,96,384]{2,1,0:T(8,128)} %shard_map.76), calls=%async_computation.1 | async-start | bytes 1179648 | tf_op jit(solution)/shard_map/all_to_all | solution.py:246
  23.0 5.1 %collective-permute-done.3 = f32[96,384]{1,0:T(8,128)S(1)} collective-permute-done((f32[96,384]{1,0:T(8,128)S(1)}, f32[96,384]{1,0:T(8,128)S(1)}, u32[]{:S(2)}, u32[]{:S(2)}) %collective-permute-start.3) | collective-permute-done | bytes 147488 | tf_op jit(solution)/shard_map/ppermute | solution.py:25
  28.2 2.8 %collective-permute-start.11 = (f32[4,96,384]{2,1,0:T(8,128)S(1)}, f32[4,96,384]{2,1,0:T(8,128)S(1)}, u32[]{:S(2)}, u32[]{:S(2)}) collective-permute-start(f32[4,96,384]{2,1,0:T(8,128)S(1)} %pad_maximum_fusion.1.refs_5_), channel_id=1, source_target_pairs={{0,48},{16,0},{32,16},{48,32},{1,49},{17,1},{33,17},{49,33},{2,50}... | collective-permute-start | bytes 1769480 | tf_op jit(solution)/shard_map/ppermute | solution.py:25
  31.6 4.6 %collective-permute-start.5 = (f32[4,96,384]{2,1,0:T(8,128)S(1)}, f32[4,96,384]{2,1,0:T(8,128)S(1)}, u32[]{:S(2)}, u32[]{:S(2)}) collective-permute-start(f32[4,96,384]{2,1,0:T(8,128)S(1)} %all-to-all-done.1.refs_0_), channel_id=1, source_target_pairs={{0,4},{4,0},{1,5},{5,1},{2,6},{6,2},{3,7},{7,3},{8,12},{12,8},{9,1... | collective-permute-start | bytes 1769480 | tf_op jit(solution)/shard_map/ppermute | solution.py:25
  36.2 3.0 %collective-permute-start.7 = (f32[2,96,384]{2,1,0:T(8,128)S(1)}, f32[2,96,384]{2,1,0:T(8,128)S(1)}, u32[]{:S(2)}, u32[]{:S(2)}) collective-permute-start(f32[2,96,384]{2,1,0:T(8,128)S(1)} %pad_maximum_fusion.2.refs_0_), channel_id=1, source_target_pairs={{0,3},{1,0},{2,1},{3,2},{4,7},{5,4},{6,5},{7,6},{8,11},{9,8},{10,9... | collective-permute-start | bytes 884744 | tf_op jit(solution)/shard_map/ppermute | solution.py:25
  39.2 4.6 %collective-permute-done.11.refs_7_ = f32[4,96,384]{2,1,0:T(8,128)S(1)} collective-permute-done((f32[4,96,384]{2,1,0:T(8,128)S(1)}, f32[4,96,384]{2,1,0:T(8,128)S(1)}, u32[]{:S(2)}, u32[]{:S(2)}) %collective-permute-start.11) | collective-permute-done | bytes 589856 | tf_op jit(solution)/shard_map/ppermute | solution.py:25
  43.7 3.4 %collective-permute-start.13 = (f32[2,96,384]{2,1,0:T(8,128)S(1)}, f32[2,96,384]{2,1,0:T(8,128)S(1)}, u32[]{:S(2)}, u32[]{:S(2)}) collective-permute-start(f32[2,96,384]{2,1,0:T(8,128)S(1)} %slice.51), channel_id=1, source_target_pairs={{0,48},{16,0},{32,16},{48,32},{1,49},{17,1},{33,17},{49,33},{2,50}... | collective-permute-start | bytes 884744 | tf_op jit(solution)/shard_map/ppermute | solution.py:25
  47.3 3.0 %collective-permute-start.9 = (f32[1,96,384]{2,1,0:T(8,128)S(1)}, f32[1,96,384]{2,1,0:T(8,128)S(1)}, u32[]{:S(2)}, u32[]{:S(2)}) collective-permute-start(f32[1,96,384]{2,1,0:T(8,128)S(1)} %slice.49), channel_id=1, source_target_pairs={{0,3},{1,0},{2,1},{3,2},{4,7},{5,4},{6,5},{7,6},{8,11},{9,8},{10,9... | collective-permute-start | bytes 442376 | tf_op jit(solution)/shard_map/ppermute | solution.py:25
  52.4 3.7 %collective-permute-done.8.refs_3_ = f32[1,96,384]{2,1,0:T(8,128)S(1)} collective-permute-done((f32[1,96,384]{2,1,0:T(8,128)S(1)}, f32[1,96,384]{2,1,0:T(8,128)S(1)}, u32[]{:S(2)}, u32[]{:S(2)}) %collective-permute-start.8) | collective-permute-done | bytes 147488 | tf_op jit(solution)/shard_map/ppermute | solution.py:25
  60.3 2.5 %shard_map.78 = (f32[96,384]{1,0:T(8,128)S(1)}, f32[96,384]{1,0:T(8,128)S(1)}, f32[16,96,384]{2,1,0:T(8,128)S(1)}) custom-call(s32[5]{0:T(128)S(1)} %stack.74.place, f32[2,96,384]{2,1,0:T(8,128)S(1)} %copy-done.7, f32[2,96,384]{2,1,0:T(8,128)S(1)} %collective-permute-done.6.refs_1_, f32[2,96,384]{2,1,0:T(8,128)S(1)} %collective-permute-done.7.refs_2_, ...), custom_call_target="tpu_custom_call" | custom-call | tf_op jit(solution)/shard_map/pallas_call | solution.py:43
  63.4 2.8 %collective-permute-start.14 = (f32[96,384]{1,0:T(8,128)S(1)}, f32[96,384]{1,0:T(8,128)S(1)}, u32[]{:S(2)}, u32[]{:S(2)}) collective-permute-start(f32[96,384]{1,0:T(8,128)S(1)} %get-tuple-element.42), channel_id=1, source_target_pairs={{0,8},{8,0},{1,9},{9,1},{2,10},{10,2},{3,11},{11,3},{4,12},{12,4},... | collective-permute-start | bytes 442376 | tf_op jit(solution)/shard_map/ppermute | solution.py:25
  72.2 3.9 %collective-permute-start.19 = (f32[96,384]{1,0:T(8,128)S(1)}, f32[96,384]{1,0:T(8,128)S(1)}, u32[]{:S(2)}, u32[]{:S(2)}) collective-permute-start(f32[96,384]{1,0:T(8,128)S(1)} %add.54.refs_2_), channel_id=1, source_target_pairs={{0,32},{16,48},{32,0},{48,16},{1,33},{17,49},{33,1},{49,17},{2,34}... | collective-permute-start | bytes 442376 | tf_op jit(solution)/shard_map/ppermute | solution.py:25
  77.4 2.5 %shard_map.79 = (bf16[4,4,192,192]{3,2,1,0:T(8,128)(2,1)S(1)}, bf16[4,4,192,192]{3,2,1,0:T(8,128)(2,1)S(1)}, bf16[4,4,192,192]{3,2,1,0:T(8,128)(2,1)S(1)}, bf16[4,4,192,192]{3,2,1,0:T(8,128)(2,1)S(1)}) custom-call(s32[5]{0:T(128)S(1)} %stack.74.place, f32[4,96,384]{2,1,0:T(8,128)S(1)} %all-to-all-done.1.refs_0_, ...), custom_call_target="tpu_custom_call" | custom-call | tf_op jit(solution)/shard_map/pallas_call | solution.py:43
  79.9 2.9 %collective-permute-done.19.refs_4_ = f32[96,384]{1,0:T(8,128)S(1)} collective-permute-done((f32[96,384]{1,0:T(8,128)S(1)}, f32[96,384]{1,0:T(8,128)S(1)}, u32[]{:S(2)}, u32[]{:S(2)}) %collective-permute-start.19) | collective-permute-done | bytes 147488 | tf_op jit(solution)/shard_map/ppermute | solution.py:25
  82.8 2.1 %shard_map.81 = (f32[96,384]{1,0:T(8,128)S(1)}, f32[96,384]{1,0:T(8,128)S(1)}, f32[96,384]{1,0:T(8,128)S(1)}, f32[96,384]{1,0:T(8,128)S(1)}) custom-call(s32[5]{0:T(128)S(1)} %stack.74.place, bf16[4,4,192,192]{3,2,1,0:T(8,128)(2,1)S(1)} %get-tuple-element.46.refs_0_, bf16[4,4,192,192]{3,2,1,0:T(8,128)(2,1)S(1)} %get-tuple-element.47.refs_1_, ...), custom_call_target="tpu_custom_call" | custom-call | tf_op jit(solution)/shard_map/pallas_call | solution.py:43
  84.9 2.4 %collective-permute-start.21 = (f32[96,384]{1,0:T(8,128)S(1)}, f32[96,384]{1,0:T(8,128)S(1)}, u32[]{:S(2)}, u32[]{:S(2)}) collective-permute-start(f32[96,384]{1,0:T(8,128)S(1)} %get-tuple-element.56), channel_id=1, source_target_pairs={{0,64},{64,128},{128,192},{192,0},{1,65},{65,129},{129,193},{193,1... | collective-permute-start | bytes 442376 | tf_op jit(solution)/shard_map/ppermute | solution.py:25
  87.4 3.0 %collective-permute-start.22 = (f32[96,384]{1,0:T(8,128)S(1)}, f32[96,384]{1,0:T(8,128)S(1)}, u32[]{:S(2)}, u32[]{:S(2)}) collective-permute-start(f32[96,384]{1,0:T(8,128)S(1)} %get-tuple-element.57), channel_id=1, source_target_pairs={{0,128},{64,192},{128,0},{192,64},{1,129},{65,193},{129,1},{193,65... | collective-permute-start | bytes 442376 | tf_op jit(solution)/shard_map/ppermute | solution.py:25
  91.3 8.6 %collective-permute-done.22 = f32[96,384]{1,0:T(8,128)S(1)} collective-permute-done((f32[96,384]{1,0:T(8,128)S(1)}, f32[96,384]{1,0:T(8,128)S(1)}, u32[]{:S(2)}, u32[]{:S(2)}) %collective-permute-start.22) | collective-permute-done | bytes 147488 | tf_op jit(solution)/shard_map/ppermute | solution.py:25
  99.9 2.7 %collective-permute-done.23 = f32[96,384]{1,0:T(8,128)S(1)} collective-permute-done((f32[96,384]{1,0:T(8,128)S(1)}, f32[96,384]{1,0:T(8,128)S(1)}, u32[]{:S(2)}, u32[]{:S(2)}) %collective-permute-start.23) | collective-permute-done | bytes 147488 | tf_op jit(solution)/shard_map/ppermute | solution.py:25
  105.0 2.8 %shard_map.80 = (bf16[8,384,384]{2,1,0:T(8,128)(2,1)S(1)}, bf16[8,384,384]{2,1,0:T(8,128)(2,1)S(1)}) custom-call(s32[5]{0:T(128)S(1)} %stack.74.place, f32[16,96,384]{2,1,0:T(8,128)S(1)} %get-tuple-element.48.own, f32[16,96,384]{2,1,0:T(8,128)} %collective-permute-done.16.away), custom_call_target="tpu_custom_call" | custom-call | tf_op jit(solution)/shard_map/pallas_call | solution.py:43
  107.8 6.8 %collective-permute-done.25.refs_4_ = f32[96,384]{1,0:T(8,128)S(1)} collective-permute-done((f32[96,384]{1,0:T(8,128)S(1)}, f32[96,384]{1,0:T(8,128)S(1)}, u32[]{:S(2)}, u32[]{:S(2)}) %collective-permute-start.25) | collective-permute-done | bytes 147488 | tf_op jit(solution)/shard_map/ppermute | solution.py:25
  114.6 3.2 %collective-permute-done.24.refs_3_ = f32[96,384]{1,0:T(8,128)S(1)} collective-permute-done((f32[96,384]{1,0:T(8,128)S(1)}, f32[96,384]{1,0:T(8,128)S(1)}, u32[]{:S(2)}, u32[]{:S(2)}) %collective-permute-start.24) | collective-permute-done | bytes 147488 | tf_op jit(solution)/shard_map/ppermute | solution.py:25
  117.8 2.1 %shard_map.82 = (f32[96,384]{1,0:T(8,128)S(1)}, f32[96,384]{1,0:T(8,128)S(1)}, f32[96,384]{1,0:T(8,128)S(1)}, f32[96,384]{1,0:T(8,128)S(1)}) custom-call(s32[5]{0:T(128)S(1)} %stack.74.place, bf16[4,4,192,192]{3,2,1,0:T(8,128)(2,1)S(1)} %get-tuple-element.51.refs_0_, bf16[4,4,192,192]{3,2,1,0:T(8,128)(2,1)S(1)} %get-tuple-element.52.refs_1_, ...), custom_call_target="tpu_custom_call" | custom-call | tf_op jit(solution)/shard_map/pallas_call | solution.py:43
  120.4 3.4 %collective-permute-start.28 = (f32[96,384]{1,0:T(8,128)S(1)}, f32[96,384]{1,0:T(8,128)S(1)}, u32[]{:S(2)}, u32[]{:S(2)}) collective-permute-start(f32[96,384]{1,0:T(8,128)S(1)} %get-tuple-element.61), channel_id=1, source_target_pairs={{0,32},{16,48},{32,0},{48,16},{1,33},{17,49},{33,1},{49,17},{2,34}... | collective-permute-start | bytes 442376 | tf_op jit(solution)/shard_map/ppermute | solution.py:25
  123.9 2.3 %collective-permute-done.27 = f32[96,384]{1,0:T(8,128)S(1)} collective-permute-done((f32[96,384]{1,0:T(8,128)S(1)}, f32[96,384]{1,0:T(8,128)S(1)}, u32[]{:S(2)}, u32[]{:S(2)}) %collective-permute-start.27) | collective-permute-done | bytes 147488 | tf_op jit(solution)/shard_map/ppermute | solution.py:25
  126.2 4.3 %collective-permute-done.28 = f32[96,384]{1,0:T(8,128)S(1)} collective-permute-done((f32[96,384]{1,0:T(8,128)S(1)}, f32[96,384]{1,0:T(8,128)S(1)}, u32[]{:S(2)}, u32[]{:S(2)}) %collective-permute-start.28) | collective-permute-done | bytes 147488 | tf_op jit(solution)/shard_map/ppermute | solution.py:25
  135.1 2.1 %collective-permute-start.35 = (f32[96,384]{1,0:T(8,128)S(1)}, f32[96,384]{1,0:T(8,128)S(1)}, u32[]{:S(2)}, u32[]{:S(2)}) collective-permute-start(f32[96,384]{1,0:T(8,128)S(1)} %get-tuple-element.71), channel_id=1, source_target_pairs={{0,2},{1,3},{2,0},{3,1},{4,6},{5,7},{6,4},{7,5},{8,10},{9,11},{10,... | collective-permute-start | bytes 442376 | tf_op jit(solution)/shard_map/ppermute | solution.py:25
  145.6 4.6 %collective-permute-start.37 = (f32[96,384]{1,0:T(8,128)S(1)}, f32[96,384]{1,0:T(8,128)S(1)}, u32[]{:S(2)}, u32[]{:S(2)}) collective-permute-start(f32[96,384]{1,0:T(8,128)S(1)} %add_add_fusion), channel_id=1, source_target_pairs={{0,4},{4,0},{1,5},{5,1},{2,6},{6,2},{3,7},{7,3},{8,12},{12,8},{9,1... | collective-permute-start | bytes 442376 | tf_op jit(solution)/shard_map/ppermute | solution.py:25
  151.4 6.7 %collective-permute-done.37 = f32[96,384]{1,0:T(8,128)S(1)} collective-permute-done((f32[96,384]{1,0:T(8,128)S(1)}, f32[96,384]{1,0:T(8,128)S(1)}, u32[]{:S(2)}, u32[]{:S(2)}) %collective-permute-start.37) | collective-permute-done | bytes 147488 | tf_op jit(solution)/shard_map/ppermute | solution.py:25
  (111 shorter events, 40.5 us)
Async XLA Ops:
  2.5 14.8 %all-to-all-start = ((f32[4,96,384]{2,1,0:T(8,128)}), f32[4,96,384]{2,1,0:T(8,128)S(1)}, u32[]{:S(2)}, u32[]{:S(2)}) async-start(f32[4,96,384]{2,1,0:T(8,128)} %broadcast_in_dim.2), calls=%async_computation | async-start | bytes 1179648 | tf_op jit(solution)/shard_map/all_to_all | solution.py:200
  7.5 15.5 %collective-permute-start.2 = (f32[96,384]{1,0:T(8,128)S(1)}, f32[96,384]{1,0:T(8,128)S(1)}, u32[]{:S(2)}, u32[]{:S(2)}) collective-permute-start(f32[96,384]{1,0:T(8,128)S(1)} %copy-done.12), channel_id=1, source_target_pairs={{0,64},{64,128},{128,192},{192,0},{1,65},{65,129},{129,193},{193,1... | collective-permute-start | bytes 442376 | tf_op jit(solution)/shard_map/ppermute | solution.py:25
  9.1 13.9 %collective-permute-start.4 = (f32[96,384]{1,0:T(8,128)S(1)}, f32[96,384]{1,0:T(8,128)S(1)}, u32[]{:S(2)}, u32[]{:S(2)}) collective-permute-start(f32[96,384]{1,0:T(8,128)S(1)} %copy-done.12), channel_id=1, source_target_pairs={{0,192},{64,0},{128,64},{192,128},{1,193},{65,1},{129,65},{193,129... | collective-permute-start | bytes 442376 | tf_op jit(solution)/shard_map/ppermute | solution.py:25
  9.1 19.0 %collective-permute-start.3 = (f32[96,384]{1,0:T(8,128)S(1)}, f32[96,384]{1,0:T(8,128)S(1)}, u32[]{:S(2)}, u32[]{:S(2)}) collective-permute-start(f32[96,384]{1,0:T(8,128)S(1)} %copy-done.12), channel_id=1, source_target_pairs={{0,128},{64,192},{128,0},{192,64},{1,129},{65,193},{129,1},{193,65... | collective-permute-start | bytes 442376 | tf_op jit(solution)/shard_map/ppermute | solution.py:25
  12.8 15.4 %collective-permute-start.1 = (f32[96,384]{1,0:T(8,128)S(1)}, f32[96,384]{1,0:T(8,128)S(1)}, u32[]{:S(2)}, u32[]{:S(2)}) collective-permute-start(f32[96,384]{1,0:T(8,128)S(1)} %shard_map.77), channel_id=1, source_target_pairs={{0,4},{4,0},{1,5},{5,1},{2,6},{6,2},{3,7},{7,3},{8,12},{12,8},{9,1... | collective-permute-start | bytes 442376 | tf_op jit(solution)/shard_map/ppermute | solution.py:25
  18.8 12.8 %all-to-all-start.1 = ((f32[4,96,384]{2,1,0:T(8,128)}), f32[4,96,384]{2,1,0:T(8,128)S(1)}, u32[]{:S(2)}, u32[]{:S(2)}) async-start(f32[4,96,384]{2,1,0:T(8,128)} %shard_map.76), calls=%async_computation.1 | async-start | bytes 1179648 | tf_op jit(solution)/shard_map/all_to_all | solution.py:246
  28.2 15.5 %collective-permute-start.11 = (f32[4,96,384]{2,1,0:T(8,128)S(1)}, f32[4,96,384]{2,1,0:T(8,128)S(1)}, u32[]{:S(2)}, u32[]{:S(2)}) collective-permute-start(f32[4,96,384]{2,1,0:T(8,128)S(1)} %pad_maximum_fusion.1.refs_5_), channel_id=1, source_target_pairs={{0,48},{16,0},{32,16},{48,32},{1,49},{17,1},{33,17},{49,33},{2,50}... | collective-permute-start | bytes 1769480 | tf_op jit(solution)/shard_map/ppermute | solution.py:25
  31.0 16.1 %collective-permute-start.10 = (f32[4,96,384]{2,1,0:T(8,128)S(1)}, f32[4,96,384]{2,1,0:T(8,128)S(1)}, u32[]{:S(2)}, u32[]{:S(2)}) collective-permute-start(f32[4,96,384]{2,1,0:T(8,128)S(1)} %pad_maximum_fusion.1.refs_5_), channel_id=1, source_target_pairs={{0,16},{16,32},{32,48},{48,0},{1,17},{17,33},{33,49},{49,1},{2,18}... | collective-permute-start | bytes 1769480 | tf_op jit(solution)/shard_map/ppermute | solution.py:25
  31.6 31.8 %collective-permute-start.5 = (f32[4,96,384]{2,1,0:T(8,128)S(1)}, f32[4,96,384]{2,1,0:T(8,128)S(1)}, u32[]{:S(2)}, u32[]{:S(2)}) collective-permute-start(f32[4,96,384]{2,1,0:T(8,128)S(1)} %all-to-all-done.1.refs_0_), channel_id=1, source_target_pairs={{0,4},{4,0},{1,5},{5,1},{2,6},{6,2},{3,7},{7,3},{8,12},{12,8},{9,1... | collective-permute-start | bytes 1769480 | tf_op jit(solution)/shard_map/ppermute | solution.py:25
  36.2 11.1 %collective-permute-start.7 = (f32[2,96,384]{2,1,0:T(8,128)S(1)}, f32[2,96,384]{2,1,0:T(8,128)S(1)}, u32[]{:S(2)}, u32[]{:S(2)}) collective-permute-start(f32[2,96,384]{2,1,0:T(8,128)S(1)} %pad_maximum_fusion.2.refs_0_), channel_id=1, source_target_pairs={{0,3},{1,0},{2,1},{3,2},{4,7},{5,4},{6,5},{7,6},{8,11},{9,8},{10,9... | collective-permute-start | bytes 884744 | tf_op jit(solution)/shard_map/ppermute | solution.py:25
  39.2 11.2 %collective-permute-start.6 = (f32[2,96,384]{2,1,0:T(8,128)S(1)}, f32[2,96,384]{2,1,0:T(8,128)S(1)}, u32[]{:S(2)}, u32[]{:S(2)}) collective-permute-start(f32[2,96,384]{2,1,0:T(8,128)S(1)} %pad_maximum_fusion.2.refs_0_), channel_id=1, source_target_pairs={{0,1},{1,2},{2,3},{3,0},{4,5},{5,6},{6,7},{7,4},{8,9},{9,10},{10,1... | collective-permute-start | bytes 884744 | tf_op jit(solution)/shard_map/ppermute | solution.py:25
  43.7 12.4 %collective-permute-start.13 = (f32[2,96,384]{2,1,0:T(8,128)S(1)}, f32[2,96,384]{2,1,0:T(8,128)S(1)}, u32[]{:S(2)}, u32[]{:S(2)}) collective-permute-start(f32[2,96,384]{2,1,0:T(8,128)S(1)} %slice.51), channel_id=1, source_target_pairs={{0,48},{16,0},{32,16},{48,32},{1,49},{17,1},{33,17},{49,33},{2,50}... | collective-permute-start | bytes 884744 | tf_op jit(solution)/shard_map/ppermute | solution.py:25
  47.2 9.0 %collective-permute-start.12 = (f32[2,96,384]{2,1,0:T(8,128)S(1)}, f32[2,96,384]{2,1,0:T(8,128)S(1)}, u32[]{:S(2)}, u32[]{:S(2)}) collective-permute-start(f32[2,96,384]{2,1,0:T(8,128)S(1)} %slice.50), channel_id=1, source_target_pairs={{0,16},{16,32},{32,48},{48,0},{1,17},{17,33},{33,49},{49,1},{2,18}... | collective-permute-start | bytes 884744 | tf_op jit(solution)/shard_map/ppermute | solution.py:25
  66.2 38.8 %collective-permute-start.16 = (f32[16,96,384]{2,1,0:T(8,128)S(1)}, f32[16,96,384]{2,1,0:T(8,128)}, u32[]{:S(2)}, u32[]{:S(2)}) collective-permute-start(f32[16,96,384]{2,1,0:T(8,128)S(1)} %get-tuple-element.48.own), channel_id=1, source_target_pairs={{0,8},{8,0},{1,9},{9,1},{2,10},{10,2},{3,11},{11,3},{4,12},{12,4},... | collective-permute-start | bytes 7077896 | tf_op jit(solution)/shard_map/ppermute | solution.py:25
  69.1 6.9 %collective-permute-start.15 = (f32[2,4,96,384]{3,2,1,0:T(8,128)}, f32[2,4,96,384]{3,2,1,0:T(8,128)}, u32[]{:S(2)}, u32[]{:S(2)}) collective-permute-start(f32[2,4,96,384]{3,2,1,0:T(8,128)} %pad_maximum_fusion), channel_id=1, source_target_pairs={{0,8},{8,0},{1,9},{9,1},{2,10},{10,2},{3,11},{11,3},{4,12},{12,4},... | collective-permute-start | bytes 3538952 | tf_op jit(solution)/shard_map/ppermute | solution.py:25
  70.7 20.1 %collective-permute-start.17 = (f32[2,96,192]{2,1,0:T(8,128)S(1)}, f32[2,96,192]{2,1,0:T(8,128)S(1)}, u32[]{:S(2)}, u32[]{:S(2)}) collective-permute-start(f32[2,96,192]{2,1,0:T(8,128)S(1)} %fusion.12), channel_id=1, source_target_pairs={{0,8},{8,0},{1,9},{9,1},{2,10},{10,2},{3,11},{11,3},{4,12},{12,4},... | collective-permute-start | bytes 442376 | tf_op jit(solution)/shard_map/ppermute | solution.py:25
  71.9 8.0 %collective-permute-start.20 = (f32[96,384]{1,0:T(8,128)S(1)}, f32[96,384]{1,0:T(8,128)S(1)}, u32[]{:S(2)}, u32[]{:S(2)}) collective-permute-start(f32[96,384]{1,0:T(8,128)S(1)} %add.54.refs_2_), channel_id=1, source_target_pairs={{0,16},{16,32},{32,48},{48,0},{1,17},{17,33},{33,49},{49,1},{2,18}... | collective-permute-start | bytes 442376 | tf_op jit(solution)/shard_map/ppermute | solution.py:25
  72.2 10.6 %collective-permute-start.19 = (f32[96,384]{1,0:T(8,128)S(1)}, f32[96,384]{1,0:T(8,128)S(1)}, u32[]{:S(2)}, u32[]{:S(2)}) collective-permute-start(f32[96,384]{1,0:T(8,128)S(1)} %add.54.refs_2_), channel_id=1, source_target_pairs={{0,32},{16,48},{32,0},{48,16},{1,33},{17,49},{33,1},{49,17},{2,34}... | collective-permute-start | bytes 442376 | tf_op jit(solution)/shard_map/ppermute | solution.py:25
  76.1 6.8 %collective-permute-start.18 = (f32[96,384]{1,0:T(8,128)S(1)}, f32[96,384]{1,0:T(8,128)S(1)}, u32[]{:S(2)}, u32[]{:S(2)}) collective-permute-start(f32[96,384]{1,0:T(8,128)S(1)} %add.54.refs_2_), channel_id=1, source_target_pairs={{0,48},{16,0},{32,16},{48,32},{1,49},{17,1},{33,17},{49,33},{2,50}... | collective-permute-start | bytes 442376 | tf_op jit(solution)/shard_map/ppermute | solution.py:25
  87.4 12.5 %collective-permute-start.22 = (f32[96,384]{1,0:T(8,128)S(1)}, f32[96,384]{1,0:T(8,128)S(1)}, u32[]{:S(2)}, u32[]{:S(2)}) collective-permute-start(f32[96,384]{1,0:T(8,128)S(1)} %get-tuple-element.57), channel_id=1, source_target_pairs={{0,128},{64,192},{128,0},{192,64},{1,129},{65,193},{129,1},{193,65... | collective-permute-start | bytes 442376 | tf_op jit(solution)/shard_map/ppermute | solution.py:25
  90.4 12.2 %collective-permute-start.23 = (f32[96,384]{1,0:T(8,128)S(1)}, f32[96,384]{1,0:T(8,128)S(1)}, u32[]{:S(2)}, u32[]{:S(2)}) collective-permute-start(f32[96,384]{1,0:T(8,128)S(1)} %get-tuple-element.58), channel_id=1, source_target_pairs={{0,192},{64,0},{128,64},{192,128},{1,193},{65,1},{129,65},{193,129... | collective-permute-start | bytes 442376 | tf_op jit(solution)/shard_map/ppermute | solution.py:25
  103.2 11.4 %collective-permute-start.25 = (f32[96,384]{1,0:T(8,128)S(1)}, f32[96,384]{1,0:T(8,128)S(1)}, u32[]{:S(2)}, u32[]{:S(2)}) collective-permute-start(f32[96,384]{1,0:T(8,128)S(1)} %get-tuple-element.75.refs_2_), channel_id=1, source_target_pairs={{0,128},{64,192},{128,0},{192,64},{1,129},{65,193},{129,1},{193,65... | collective-permute-start | bytes 442376 | tf_op jit(solution)/shard_map/ppermute | solution.py:25
  103.6 14.2 %collective-permute-start.24 = (f32[96,384]{1,0:T(8,128)S(1)}, f32[96,384]{1,0:T(8,128)S(1)}, u32[]{:S(2)}, u32[]{:S(2)}) collective-permute-start(f32[96,384]{1,0:T(8,128)S(1)} %get-tuple-element.75.refs_2_), channel_id=1, source_target_pairs={{0,192},{64,0},{128,64},{192,128},{1,193},{65,1},{129,65},{193,129... | collective-permute-start | bytes 442376 | tf_op jit(solution)/shard_map/ppermute | solution.py:25
  120.4 10.0 %collective-permute-start.28 = (f32[96,384]{1,0:T(8,128)S(1)}, f32[96,384]{1,0:T(8,128)S(1)}, u32[]{:S(2)}, u32[]{:S(2)}) collective-permute-start(f32[96,384]{1,0:T(8,128)S(1)} %get-tuple-element.61), channel_id=1, source_target_pairs={{0,32},{16,48},{32,0},{48,16},{1,33},{17,49},{33,1},{49,17},{2,34}... | collective-permute-start | bytes 442376 | tf_op jit(solution)/shard_map/ppermute | solution.py:25
  135.0 7.0 %collective-permute-start.34 = (f32[96,384]{1,0:T(8,128)S(1)}, f32[96,384]{1,0:T(8,128)S(1)}, u32[]{:S(2)}, u32[]{:S(2)}) collective-permute-start(f32[96,384]{1,0:T(8,128)S(1)} %get-tuple-element.70), channel_id=1, source_target_pairs={{0,1},{1,2},{2,3},{3,0},{4,5},{5,6},{6,7},{7,4},{8,9},{9,10},{10,1... | collective-permute-start | bytes 442376 | tf_op jit(solution)/shard_map/ppermute | solution.py:25
  135.1 8.9 %collective-permute-start.35 = (f32[96,384]{1,0:T(8,128)S(1)}, f32[96,384]{1,0:T(8,128)S(1)}, u32[]{:S(2)}, u32[]{:S(2)}) collective-permute-start(f32[96,384]{1,0:T(8,128)S(1)} %get-tuple-element.71), channel_id=1, source_target_pairs={{0,2},{1,3},{2,0},{3,1},{4,6},{5,7},{6,4},{7,5},{8,10},{9,11},{10,... | collective-permute-start | bytes 442376 | tf_op jit(solution)/shard_map/ppermute | solution.py:25
  137.2 8.3 %collective-permute-start.36 = (f32[96,384]{1,0:T(8,128)S(1)}, f32[96,384]{1,0:T(8,128)S(1)}, u32[]{:S(2)}, u32[]{:S(2)}) collective-permute-start(f32[96,384]{1,0:T(8,128)S(1)} %get-tuple-element.72), channel_id=1, source_target_pairs={{0,3},{1,0},{2,1},{3,2},{4,7},{5,4},{6,5},{7,6},{8,11},{9,8},{10,9... | collective-permute-start | bytes 442376 | tf_op jit(solution)/shard_map/ppermute | solution.py:25
  138.5 11.7 %collective-permute-start.38 = (f32[2,96,192]{2,1,0:T(8,128)S(1)}, f32[2,96,192]{2,1,0:T(8,128)S(1)}, u32[]{:S(2)}, u32[]{:S(2)}) collective-permute-start(f32[2,96,192]{2,1,0:T(8,128)S(1)} %fusion.14), channel_id=1, source_target_pairs={{0,8},{8,0},{1,9},{9,1},{2,10},{10,2},{3,11},{11,3},{4,12},{12,4},... | collective-permute-start | bytes 442376 | tf_op jit(solution)/shard_map/ppermute | solution.py:25
  141.6 9.5 %collective-permute-start.31 = (f32[96,384]{1,0:T(8,128)S(1)}, f32[96,384]{1,0:T(8,128)S(1)}, u32[]{:S(2)}, u32[]{:S(2)}) collective-permute-start(f32[96,384]{1,0:T(8,128)S(1)} %get-tuple-element.66), channel_id=1, source_target_pairs={{0,1},{1,2},{2,3},{3,0},{4,5},{5,6},{6,7},{7,4},{8,9},{9,10},{10,1... | collective-permute-start | bytes 442376 | tf_op jit(solution)/shard_map/ppermute | solution.py:25
  142.0 9.2 %collective-permute-start.32 = (f32[96,384]{1,0:T(8,128)S(1)}, f32[96,384]{1,0:T(8,128)S(1)}, u32[]{:S(2)}, u32[]{:S(2)}) collective-permute-start(f32[96,384]{1,0:T(8,128)S(1)} %get-tuple-element.67), channel_id=1, source_target_pairs={{0,2},{1,3},{2,0},{3,1},{4,6},{5,7},{6,4},{7,5},{8,10},{9,11},{10,... | collective-permute-start | bytes 442376 | tf_op jit(solution)/shard_map/ppermute | solution.py:25
  144.0 7.4 %collective-permute-start.33 = (f32[96,384]{1,0:T(8,128)S(1)}, f32[96,384]{1,0:T(8,128)S(1)}, u32[]{:S(2)}, u32[]{:S(2)}) collective-permute-start(f32[96,384]{1,0:T(8,128)S(1)} %get-tuple-element.68), channel_id=1, source_target_pairs={{0,3},{1,0},{2,1},{3,2},{4,7},{5,4},{6,5},{7,6},{8,11},{9,8},{10,9... | collective-permute-start | bytes 442376 | tf_op jit(solution)/shard_map/ppermute | solution.py:25
  145.6 12.5 %collective-permute-start.37 = (f32[96,384]{1,0:T(8,128)S(1)}, f32[96,384]{1,0:T(8,128)S(1)}, u32[]{:S(2)}, u32[]{:S(2)}) collective-permute-start(f32[96,384]{1,0:T(8,128)S(1)} %add_add_fusion), channel_id=1, source_target_pairs={{0,4},{4,0},{1,5},{5,1},{2,6},{6,2},{3,7},{7,3},{8,12},{12,8},{9,1... | collective-permute-start | bytes 442376 | tf_op jit(solution)/shard_map/ppermute | solution.py:25
  (23 other events, 158.2 us)

commit v2 on v1

--- a/solution.py
+++ b/solution.py
@@ -131,8 +131,8 @@
 
 
 def left_kernel(place, *refs):
-    owns, aways = refs[:2], refs[2:4]
-    high, low, t_high, t_low = refs[4:]
+    owns, aways = refs[:2], refs[2]
+    high, low, t_high, t_low = refs[3:]
     rows, half = owns[0].shape[1], owns[0].shape[2] // 2
     first = place[C] == 0
     for r in range(2):
@@ -142,7 +142,7 @@
             for d in range(4):
                 at = lax.rem(place[Y] + d, 4)
                 lanes = slice(half * t, half * (t + 1))
-                mine, theirs = owns[r][at, :, lanes], aways[r][at, :, lanes]
+                mine, theirs = owns[r][at, :, lanes], aways[r, at, :, lanes]
                 tile = jnp.concatenate(
                     [jnp.where(first, mine, theirs), jnp.where(first, theirs, mine)]
                 )
@@ -258,13 +258,15 @@
     )
     other, _ = lax.optimization_barrier((other, left_far))
     other = shift(other, "c", 1)
-    left_far, other = lax.optimization_barrier((left_far, other))
     rotated_right = mine + other
+    left_far, first_moment, second_moment, right, rotated_right = lax.optimization_barrier(
+        (left_far, first_moment, second_moment, right, rotated_right)
+    )
     both = shift(jnp.stack([left, left_far]), "c", 1)
     lefts = call(
         left_kernel,
         place,
-        [left, left_far, both[0], both[1]],
+        [left, left_far, both],
         [shape(4, 4, size, half, dtype=BF16)] * 2
         + [shape(4, 4, half, size, dtype=BF16)] * 2,
     )

time: 160 us -> 157 us (0.981)
  local copies, waits for them, and re-layouts: 8.81 us -> 6.15 us
    unnamed x28 -> x26, local copies, waits for them, and re-layouts: 5.49 us -> 4.18 us
  transfers between devices with their start and end apart: 41 -> 41, of which waited for: 18 -> 19; matrix products, arithmetic and copies ran while one was open for 4% -> 3% of each run, Pallas kernels for 9% -> 9%
where the time goes in v2:
time: 157 us; the launch traced here: 156 us
  starting transfers between devices  69 us (44%)
  waiting for transfers between devices  55.5 us (35%)
  Pallas kernels  18.5 us (12%)
  local copies, waits for them, and re-layouts  6.15 us (4%)
  other arithmetic  5.48 us (3%)
    ppermute x39, starting transfers between devices, shift(): return lax.ppermute(value, axis, [(i, (i + by) % n) for i in range(n)])  60.8 us
    ppermute x39, waiting for transfers between devices, shift(): return lax.ppermute(value, axis, [(i, (i + by) % n) for i in range(n)])  54.9 us
    pallas_call x9, Pallas kernels, call(): pl.pallas_call(kernel, out_shape=outs, in_specs=[pl.BlockSpec(memory_spac...  18.5 us
    unnamed x26, local copies, waits for them, and re-layouts  4.18 us
    all_to_all x1, starting transfers between devices, body(): left = lax.all_to_all(packs, 'y', 0, 0, tiled=True)  4.18 us
    all_to_all x1, starting transfers between devices, copies_sent(): return lax.all_to_all(copies, axis, 0, 0, tiled=True)  4.01 us
  transfers between devices with their start and end apart: 41, of which 19 were waited for; matrix products, arithmetic and copies ran while one was open for 3% of the time, Pallas kernels for 9%

profile of v2, /device:TPU:33, one launch (start us, length us, event | category | flops | bytes accessed | tf_op | source)
XLA Modules:
  0.0 155.7 jit_solution(11589778178732406958)
XLA Ops:
  0.7 1.8 %broadcast_in_dim.2 = f32[4,96,384]{2,1,0:T(8,128)} broadcast(f32[96,384]{1,0:T(8,128)} %param.8), dimensions={1,2} | broadcast | bytes 737280 | tf_op jit(solution)/shard_map/broadcast_in_dim | solution.py:199
  2.5 4.0 %all-to-all-start = ((f32[4,96,384]{2,1,0:T(8,128)}), f32[4,96,384]{2,1,0:T(8,128)S(1)}, u32[]{:S(2)}, u32[]{:S(2)}) async-start(f32[4,96,384]{2,1,0:T(8,128)} %broadcast_in_dim.2), calls=%async_computation | async-start | bytes 1179648 | tf_op jit(solution)/shard_map/all_to_all | solution.py:200
  9.1 2.8 %collective-permute-start.3 = (f32[96,384]{1,0:T(8,128)S(1)}, f32[96,384]{1,0:T(8,128)S(1)}, u32[]{:S(2)}, u32[]{:S(2)}) collective-permute-start(f32[96,384]{1,0:T(8,128)S(1)} %copy-done.12), channel_id=1, source_target_pairs={{0,128},{64,192},{128,0},{192,64},{1,129},{65,193},{129,1},{193,65... | collective-permute-start | bytes 442376 | tf_op jit(solution)/shard_map/ppermute | solution.py:25
  12.8 4.5 %collective-permute-start.1 = (f32[96,384]{1,0:T(8,128)S(1)}, f32[96,384]{1,0:T(8,128)S(1)}, u32[]{:S(2)}, u32[]{:S(2)}) collective-permute-start(f32[96,384]{1,0:T(8,128)S(1)} %shard_map.77), channel_id=1, source_target_pairs={{0,4},{4,0},{1,5},{5,1},{2,6},{6,2},{3,7},{7,3},{8,12},{12,8},{9,1... | collective-permute-start | bytes 442376 | tf_op jit(solution)/shard_map/ppermute | solution.py:25
  18.8 4.2 %all-to-all-start.1 = ((f32[4,96,384]{2,1,0:T(8,128)}), f32[4,96,384]{2,1,0:T(8,128)S(1)}, u32[]{:S(2)}, u32[]{:S(2)}) async-start(f32[4,96,384]{2,1,0:T(8,128)} %shard_map.76), calls=%async_computation.1 | async-start | bytes 1179648 | tf_op jit(solution)/shard_map/all_to_all | solution.py:246
  23.0 5.1 %collective-permute-done.3 = f32[96,384]{1,0:T(8,128)S(1)} collective-permute-done((f32[96,384]{1,0:T(8,128)S(1)}, f32[96,384]{1,0:T(8,128)S(1)}, u32[]{:S(2)}, u32[]{:S(2)}) %collective-permute-start.3) | collective-permute-done | bytes 147488 | tf_op jit(solution)/shard_map/ppermute | solution.py:25
  28.2 2.8 %collective-permute-start.11 = (f32[4,96,384]{2,1,0:T(8,128)S(1)}, f32[4,96,384]{2,1,0:T(8,128)S(1)}, u32[]{:S(2)}, u32[]{:S(2)}) collective-permute-start(f32[4,96,384]{2,1,0:T(8,128)S(1)} %pad_maximum_fusion.1.refs_5_), channel_id=1, source_target_pairs={{0,48},{16,0},{32,16},{48,32},{1,49},{17,1},{33,17},{49,33},{2,50}... | collective-permute-start | bytes 1769480 | tf_op jit(solution)/shard_map/ppermute | solution.py:25
  31.6 4.6 %collective-permute-start.5 = (f32[4,96,384]{2,1,0:T(8,128)S(1)}, f32[4,96,384]{2,1,0:T(8,128)S(1)}, u32[]{:S(2)}, u32[]{:S(2)}) collective-permute-start(f32[4,96,384]{2,1,0:T(8,128)S(1)} %all-to-all-done.1.refs_0_), channel_id=1, source_target_pairs={{0,4},{4,0},{1,5},{5,1},{2,6},{6,2},{3,7},{7,3},{8,12},{12,8},{9,1... | collective-permute-start | bytes 1769480 | tf_op jit(solution)/shard_map/ppermute | solution.py:25
  36.2 3.0 %collective-permute-start.7 = (f32[2,96,384]{2,1,0:T(8,128)S(1)}, f32[2,96,384]{2,1,0:T(8,128)S(1)}, u32[]{:S(2)}, u32[]{:S(2)}) collective-permute-start(f32[2,96,384]{2,1,0:T(8,128)S(1)} %pad_maximum_fusion.2.refs_0_), channel_id=1, source_target_pairs={{0,3},{1,0},{2,1},{3,2},{4,7},{5,4},{6,5},{7,6},{8,11},{9,8},{10,9... | collective-permute-start | bytes 884744 | tf_op jit(solution)/shard_map/ppermute | solution.py:25
  39.1 4.6 %collective-permute-done.11.refs_7_ = f32[4,96,384]{2,1,0:T(8,128)S(1)} collective-permute-done((f32[4,96,384]{2,1,0:T(8,128)S(1)}, f32[4,96,384]{2,1,0:T(8,128)S(1)}, u32[]{:S(2)}, u32[]{:S(2)}) %collective-permute-start.11) | collective-permute-done | bytes 589856 | tf_op jit(solution)/shard_map/ppermute | solution.py:25
  43.7 3.4 %collective-permute-start.13 = (f32[2,96,384]{2,1,0:T(8,128)S(1)}, f32[2,96,384]{2,1,0:T(8,128)S(1)}, u32[]{:S(2)}, u32[]{:S(2)}) collective-permute-start(f32[2,96,384]{2,1,0:T(8,128)S(1)} %slice.43), channel_id=1, source_target_pairs={{0,48},{16,0},{32,16},{48,32},{1,49},{17,1},{33,17},{49,33},{2,50}... | collective-permute-start | bytes 884744 | tf_op jit(solution)/shard_map/ppermute | solution.py:25
  47.3 3.0 %collective-permute-start.9 = (f32[1,96,384]{2,1,0:T(8,128)S(1)}, f32[1,96,384]{2,1,0:T(8,128)S(1)}, u32[]{:S(2)}, u32[]{:S(2)}) collective-permute-start(f32[1,96,384]{2,1,0:T(8,128)S(1)} %slice.41), channel_id=1, source_target_pairs={{0,3},{1,0},{2,1},{3,2},{4,7},{5,4},{6,5},{7,6},{8,11},{9,8},{10,9... | collective-permute-start | bytes 442376 | tf_op jit(solution)/shard_map/ppermute | solution.py:25
  52.4 3.7 %collective-permute-done.8.refs_3_ = f32[1,96,384]{2,1,0:T(8,128)S(1)} collective-permute-done((f32[1,96,384]{2,1,0:T(8,128)S(1)}, f32[1,96,384]{2,1,0:T(8,128)S(1)}, u32[]{:S(2)}, u32[]{:S(2)}) %collective-permute-start.8) | collective-permute-done | bytes 147488 | tf_op jit(solution)/shard_map/ppermute | solution.py:25
  60.3 2.5 %shard_map.78 = (f32[96,384]{1,0:T(8,128)S(1)}, f32[96,384]{1,0:T(8,128)S(1)}, f32[16,96,384]{2,1,0:T(8,128)S(1)}) custom-call(s32[5]{0:T(128)S(1)} %stack.74.place, f32[2,96,384]{2,1,0:T(8,128)S(1)} %copy-done.7, f32[2,96,384]{2,1,0:T(8,128)S(1)} %collective-permute-done.6.refs_1_, f32[2,96,384]{2,1,0:T(8,128)S(1)} %collective-permute-done.7.refs_2_, ...), custom_call_target="tpu_custom_call" | custom-call | tf_op jit(solution)/shard_map/pallas_call | solution.py:43
  62.8 2.8 %collective-permute-start.14 = (f32[96,384]{1,0:T(8,128)S(1)}, f32[96,384]{1,0:T(8,128)S(1)}, u32[]{:S(2)}, u32[]{:S(2)}) collective-permute-start(f32[96,384]{1,0:T(8,128)S(1)} %get-tuple-element.47), channel_id=1, source_target_pairs={{0,8},{8,0},{1,9},{9,1},{2,10},{10,2},{3,11},{11,3},{4,12},{12,4},... | collective-permute-start | bytes 442376 | tf_op jit(solution)/shard_map/ppermute | solution.py:25
  69.2 3.9 %collective-permute-start.19 = (f32[96,384]{1,0:T(8,128)}, f32[96,384]{1,0:T(8,128)S(1)}, u32[]{:S(2)}, u32[]{:S(2)}) collective-permute-start(f32[96,384]{1,0:T(8,128)} %add.54.refs_2_), channel_id=1, source_target_pairs={{0,32},{16,48},{32,0},{48,16},{1,33},{17,49},{33,1},{49,17},{2,34}... | collective-permute-start | bytes 442376 | tf_op jit(solution)/shard_map/ppermute | solution.py:25
  75.2 3.2 %shard_map.79 = (bf16[4,4,192,192]{3,2,1,0:T(8,128)(2,1)S(1)}, bf16[4,4,192,192]{3,2,1,0:T(8,128)(2,1)S(1)}, bf16[4,4,192,192]{3,2,1,0:T(8,128)(2,1)S(1)}, bf16[4,4,192,192]{3,2,1,0:T(8,128)(2,1)S(1)}) custom-call(s32[5]{0:T(128)S(1)} %stack.74.place, f32[4,96,384]{2,1,0:T(8,128)S(1)} %all-to-all-done.1.refs_0_, ...), custom_call_target="tpu_custom_call" | custom-call | tf_op jit(solution)/shard_map/pallas_call | solution.py:43
  80.0 2.1 %shard_map.81 = (f32[96,384]{1,0:T(8,128)S(1)}, f32[96,384]{1,0:T(8,128)S(1)}, f32[96,384]{1,0:T(8,128)S(1)}, f32[96,384]{1,0:T(8,128)S(1)}) custom-call(s32[5]{0:T(128)S(1)} %stack.74.place, bf16[4,4,192,192]{3,2,1,0:T(8,128)(2,1)S(1)} %get-tuple-element.51.refs_0_, bf16[4,4,192,192]{3,2,1,0:T(8,128)(2,1)S(1)} %get-tuple-element.52.refs_1_, ...), custom_call_target="tpu_custom_call" | custom-call | tf_op jit(solution)/shard_map/pallas_call | solution.py:43
  82.1 2.4 %collective-permute-start.21 = (f32[96,384]{1,0:T(8,128)S(1)}, f32[96,384]{1,0:T(8,128)S(1)}, u32[]{:S(2)}, u32[]{:S(2)}) collective-permute-start(f32[96,384]{1,0:T(8,128)S(1)} %get-tuple-element.62), channel_id=1, source_target_pairs={{0,64},{64,128},{128,192},{192,0},{1,65},{65,129},{129,193},{193,1... | collective-permute-start | bytes 442376 | tf_op jit(solution)/shard_map/ppermute | solution.py:25
  84.6 3.0 %collective-permute-start.22 = (f32[96,384]{1,0:T(8,128)S(1)}, f32[96,384]{1,0:T(8,128)S(1)}, u32[]{:S(2)}, u32[]{:S(2)}) collective-permute-start(f32[96,384]{1,0:T(8,128)S(1)} %get-tuple-element.63), channel_id=1, source_target_pairs={{0,128},{64,192},{128,0},{192,64},{1,129},{65,193},{129,1},{193,65... | collective-permute-start | bytes 442376 | tf_op jit(solution)/shard_map/ppermute | solution.py:25
  88.4 8.6 %collective-permute-done.22 = f32[96,384]{1,0:T(8,128)S(1)} collective-permute-done((f32[96,384]{1,0:T(8,128)S(1)}, f32[96,384]{1,0:T(8,128)S(1)}, u32[]{:S(2)}, u32[]{:S(2)}) %collective-permute-start.22) | collective-permute-done | bytes 147488 | tf_op jit(solution)/shard_map/ppermute | solution.py:25
  97.1 2.7 %collective-permute-done.23 = f32[96,384]{1,0:T(8,128)S(1)} collective-permute-done((f32[96,384]{1,0:T(8,128)S(1)}, f32[96,384]{1,0:T(8,128)S(1)}, u32[]{:S(2)}, u32[]{:S(2)}) %collective-permute-start.23) | collective-permute-done | bytes 147488 | tf_op jit(solution)/shard_map/ppermute | solution.py:25
  102.0 2.7 %shard_map.80 = (bf16[8,384,384]{2,1,0:T(8,128)(2,1)S(1)}, bf16[8,384,384]{2,1,0:T(8,128)(2,1)S(1)}) custom-call(s32[5]{0:T(128)S(1)} %stack.74.place, f32[16,96,384]{2,1,0:T(8,128)S(1)} %get-tuple-element.53.own, f32[16,96,384]{2,1,0:T(8,128)} %collective-permute-done.16.away), custom_call_target="tpu_custom_call" | custom-call | tf_op jit(solution)/shard_map/pallas_call | solution.py:43
  104.7 6.9 %collective-permute-done.25.refs_4_ = f32[96,384]{1,0:T(8,128)S(1)} collective-permute-done((f32[96,384]{1,0:T(8,128)S(1)}, f32[96,384]{1,0:T(8,128)S(1)}, u32[]{:S(2)}, u32[]{:S(2)}) %collective-permute-start.25) | collective-permute-done | bytes 147488 | tf_op jit(solution)/shard_map/ppermute | solution.py:25
  111.6 3.3 %collective-permute-done.24.refs_3_ = f32[96,384]{1,0:T(8,128)S(1)} collective-permute-done((f32[96,384]{1,0:T(8,128)S(1)}, f32[96,384]{1,0:T(8,128)S(1)}, u32[]{:S(2)}, u32[]{:S(2)}) %collective-permute-start.24) | collective-permute-done | bytes 147488 | tf_op jit(solution)/shard_map/ppermute | solution.py:25
  115.0 2.1 %shard_map.82 = (f32[96,384]{1,0:T(8,128)S(1)}, f32[96,384]{1,0:T(8,128)S(1)}, f32[96,384]{1,0:T(8,128)S(1)}, f32[96,384]{1,0:T(8,128)S(1)}) custom-call(s32[5]{0:T(128)S(1)} %stack.74.place, bf16[4,4,192,192]{3,2,1,0:T(8,128)(2,1)S(1)} %get-tuple-element.56.refs_0_, bf16[4,4,192,192]{3,2,1,0:T(8,128)(2,1)S(1)} %get-tuple-element.57.refs_1_, ...), custom_call_target="tpu_custom_call" | custom-call | tf_op jit(solution)/shard_map/pallas_call | solution.py:43
  117.6 3.2 %collective-permute-start.28 = (f32[96,384]{1,0:T(8,128)S(1)}, f32[96,384]{1,0:T(8,128)S(1)}, u32[]{:S(2)}, u32[]{:S(2)}) collective-permute-start(f32[96,384]{1,0:T(8,128)S(1)} %get-tuple-element.67), channel_id=1, source_target_pairs={{0,32},{16,48},{32,0},{48,16},{1,33},{17,49},{33,1},{49,17},{2,34}... | collective-permute-start | bytes 442376 | tf_op jit(solution)/shard_map/ppermute | solution.py:25
  120.9 2.3 %collective-permute-done.27 = f32[96,384]{1,0:T(8,128)S(1)} collective-permute-done((f32[96,384]{1,0:T(8,128)S(1)}, f32[96,384]{1,0:T(8,128)S(1)}, u32[]{:S(2)}, u32[]{:S(2)}) %collective-permute-start.27) | collective-permute-done | bytes 147488 | tf_op jit(solution)/shard_map/ppermute | solution.py:25
  123.2 4.3 %collective-permute-done.28 = f32[96,384]{1,0:T(8,128)S(1)} collective-permute-done((f32[96,384]{1,0:T(8,128)S(1)}, f32[96,384]{1,0:T(8,128)S(1)}, u32[]{:S(2)}, u32[]{:S(2)}) %collective-permute-start.28) | collective-permute-done | bytes 147488 | tf_op jit(solution)/shard_map/ppermute | solution.py:25
  132.2 2.4 %collective-permute-start.35 = (f32[96,384]{1,0:T(8,128)S(1)}, f32[96,384]{1,0:T(8,128)S(1)}, u32[]{:S(2)}, u32[]{:S(2)}) collective-permute-start(f32[96,384]{1,0:T(8,128)S(1)} %get-tuple-element.77), channel_id=1, source_target_pairs={{0,2},{1,3},{2,0},{3,1},{4,6},{5,7},{6,4},{7,5},{8,10},{9,11},{10,... | collective-permute-start | bytes 442376 | tf_op jit(solution)/shard_map/ppermute | solution.py:25
  142.5 4.6 %collective-permute-start.37 = (f32[96,384]{1,0:T(8,128)S(1)}, f32[96,384]{1,0:T(8,128)S(1)}, u32[]{:S(2)}, u32[]{:S(2)}) collective-permute-start(f32[96,384]{1,0:T(8,128)S(1)} %add_add_fusion), channel_id=1, source_target_pairs={{0,4},{4,0},{1,5},{5,1},{2,6},{6,2},{3,7},{7,3},{8,12},{12,8},{9,1... | collective-permute-start | bytes 442376 | tf_op jit(solution)/shard_map/ppermute | solution.py:25
  149.3 5.7 %collective-permute-done.37 = f32[96,384]{1,0:T(8,128)S(1)} collective-permute-done((f32[96,384]{1,0:T(8,128)S(1)}, f32[96,384]{1,0:T(8,128)S(1)}, u32[]{:S(2)}, u32[]{:S(2)}) %collective-permute-start.37) | collective-permute-done | bytes 147488 | tf_op jit(solution)/shard_map/ppermute | solution.py:25
  (108 shorter events, 38.4 us)
Async XLA Ops:
  2.5 14.8 %all-to-all-start = ((f32[4,96,384]{2,1,0:T(8,128)}), f32[4,96,384]{2,1,0:T(8,128)S(1)}, u32[]{:S(2)}, u32[]{:S(2)}) async-start(f32[4,96,384]{2,1,0:T(8,128)} %broadcast_in_dim.2), calls=%async_computation | async-start | bytes 1179648 | tf_op jit(solution)/shard_map/all_to_all | solution.py:200
  7.4 15.5 %collective-permute-start.2 = (f32[96,384]{1,0:T(8,128)S(1)}, f32[96,384]{1,0:T(8,128)S(1)}, u32[]{:S(2)}, u32[]{:S(2)}) collective-permute-start(f32[96,384]{1,0:T(8,128)S(1)} %copy-done.12), channel_id=1, source_target_pairs={{0,64},{64,128},{128,192},{192,0},{1,65},{65,129},{129,193},{193,1... | collective-permute-start | bytes 442376 | tf_op jit(solution)/shard_map/ppermute | solution.py:25
  9.1 13.9 %collective-permute-start.4 = (f32[96,384]{1,0:T(8,128)S(1)}, f32[96,384]{1,0:T(8,128)S(1)}, u32[]{:S(2)}, u32[]{:S(2)}) collective-permute-start(f32[96,384]{1,0:T(8,128)S(1)} %copy-done.12), channel_id=1, source_target_pairs={{0,192},{64,0},{128,64},{192,128},{1,193},{65,1},{129,65},{193,129... | collective-permute-start | bytes 442376 | tf_op jit(solution)/shard_map/ppermute | solution.py:25
  9.1 19.0 %collective-permute-start.3 = (f32[96,384]{1,0:T(8,128)S(1)}, f32[96,384]{1,0:T(8,128)S(1)}, u32[]{:S(2)}, u32[]{:S(2)}) collective-permute-start(f32[96,384]{1,0:T(8,128)S(1)} %copy-done.12), channel_id=1, source_target_pairs={{0,128},{64,192},{128,0},{192,64},{1,129},{65,193},{129,1},{193,65... | collective-permute-start | bytes 442376 | tf_op jit(solution)/shard_map/ppermute | solution.py:25
  12.8 15.4 %collective-permute-start.1 = (f32[96,384]{1,0:T(8,128)S(1)}, f32[96,384]{1,0:T(8,128)S(1)}, u32[]{:S(2)}, u32[]{:S(2)}) collective-permute-start(f32[96,384]{1,0:T(8,128)S(1)} %shard_map.77), channel_id=1, source_target_pairs={{0,4},{4,0},{1,5},{5,1},{2,6},{6,2},{3,7},{7,3},{8,12},{12,8},{9,1... | collective-permute-start | bytes 442376 | tf_op jit(solution)/shard_map/ppermute | solution.py:25
  18.8 12.8 %all-to-all-start.1 = ((f32[4,96,384]{2,1,0:T(8,128)}), f32[4,96,384]{2,1,0:T(8,128)S(1)}, u32[]{:S(2)}, u32[]{:S(2)}) async-start(f32[4,96,384]{2,1,0:T(8,128)} %shard_map.76), calls=%async_computation.1 | async-start | bytes 1179648 | tf_op jit(solution)/shard_map/all_to_all | solution.py:246
  28.2 15.5 %collective-permute-start.11 = (f32[4,96,384]{2,1,0:T(8,128)S(1)}, f32[4,96,384]{2,1,0:T(8,128)S(1)}, u32[]{:S(2)}, u32[]{:S(2)}) collective-permute-start(f32[4,96,384]{2,1,0:T(8,128)S(1)} %pad_maximum_fusion.1.refs_5_), channel_id=1, source_target_pairs={{0,48},{16,0},{32,16},{48,32},{1,49},{17,1},{33,17},{49,33},{2,50}... | collective-permute-start | bytes 1769480 | tf_op jit(solution)/shard_map/ppermute | solution.py:25
  31.0 16.1 %collective-permute-start.10 = (f32[4,96,384]{2,1,0:T(8,128)S(1)}, f32[4,96,384]{2,1,0:T(8,128)S(1)}, u32[]{:S(2)}, u32[]{:S(2)}) collective-permute-start(f32[4,96,384]{2,1,0:T(8,128)S(1)} %pad_maximum_fusion.1.refs_5_), channel_id=1, source_target_pairs={{0,16},{16,32},{32,48},{48,0},{1,17},{17,33},{33,49},{49,1},{2,18}... | collective-permute-start | bytes 1769480 | tf_op jit(solution)/shard_map/ppermute | solution.py:25
  31.6 31.2 %collective-permute-start.5 = (f32[4,96,384]{2,1,0:T(8,128)S(1)}, f32[4,96,384]{2,1,0:T(8,128)S(1)}, u32[]{:S(2)}, u32[]{:S(2)}) collective-permute-start(f32[4,96,384]{2,1,0:T(8,128)S(1)} %all-to-all-done.1.refs_0_), channel_id=1, source_target_pairs={{0,4},{4,0},{1,5},{5,1},{2,6},{6,2},{3,7},{7,3},{8,12},{12,8},{9,1... | collective-permute-start | bytes 1769480 | tf_op jit(solution)/shard_map/ppermute | solution.py:25
  36.2 11.1 %collective-permute-start.7 = (f32[2,96,384]{2,1,0:T(8,128)S(1)}, f32[2,96,384]{2,1,0:T(8,128)S(1)}, u32[]{:S(2)}, u32[]{:S(2)}) collective-permute-start(f32[2,96,384]{2,1,0:T(8,128)S(1)} %pad_maximum_fusion.2.refs_0_), channel_id=1, source_target_pairs={{0,3},{1,0},{2,1},{3,2},{4,7},{5,4},{6,5},{7,6},{8,11},{9,8},{10,9... | collective-permute-start | bytes 884744 | tf_op jit(solution)/shard_map/ppermute | solution.py:25
  39.1 11.2 %collective-permute-start.6 = (f32[2,96,384]{2,1,0:T(8,128)S(1)}, f32[2,96,384]{2,1,0:T(8,128)S(1)}, u32[]{:S(2)}, u32[]{:S(2)}) collective-permute-start(f32[2,96,384]{2,1,0:T(8,128)S(1)} %pad_maximum_fusion.2.refs_0_), channel_id=1, source_target_pairs={{0,1},{1,2},{2,3},{3,0},{4,5},{5,6},{6,7},{7,4},{8,9},{9,10},{10,1... | collective-permute-start | bytes 884744 | tf_op jit(solution)/shard_map/ppermute | solution.py:25
  43.7 12.4 %collective-permute-start.13 = (f32[2,96,384]{2,1,0:T(8,128)S(1)}, f32[2,96,384]{2,1,0:T(8,128)S(1)}, u32[]{:S(2)}, u32[]{:S(2)}) collective-permute-start(f32[2,96,384]{2,1,0:T(8,128)S(1)} %slice.43), channel_id=1, source_target_pairs={{0,48},{16,0},{32,16},{48,32},{1,49},{17,1},{33,17},{49,33},{2,50}... | collective-permute-start | bytes 884744 | tf_op jit(solution)/shard_map/ppermute | solution.py:25
  47.2 9.0 %collective-permute-start.12 = (f32[2,96,384]{2,1,0:T(8,128)S(1)}, f32[2,96,384]{2,1,0:T(8,128)S(1)}, u32[]{:S(2)}, u32[]{:S(2)}) collective-permute-start(f32[2,96,384]{2,1,0:T(8,128)S(1)} %slice.42), channel_id=1, source_target_pairs={{0,16},{16,32},{32,48},{48,0},{1,17},{17,33},{33,49},{49,1},{2,18}... | collective-permute-start | bytes 884744 | tf_op jit(solution)/shard_map/ppermute | solution.py:25
  67.3 34.7 %collective-permute-start.16 = (f32[16,96,384]{2,1,0:T(8,128)S(1)}, f32[16,96,384]{2,1,0:T(8,128)}, u32[]{:S(2)}, u32[]{:S(2)}) collective-permute-start(f32[16,96,384]{2,1,0:T(8,128)S(1)} %get-tuple-element.53.own), channel_id=1, source_target_pairs={{0,8},{8,0},{1,9},{9,1},{2,10},{10,2},{3,11},{11,3},{4,12},{12,4},... | collective-permute-start | bytes 7077896 | tf_op jit(solution)/shard_map/ppermute | solution.py:25
  68.9 9.5 %collective-permute-start.20 = (f32[96,384]{1,0:T(8,128)}, f32[96,384]{1,0:T(8,128)S(1)}, u32[]{:S(2)}, u32[]{:S(2)}) collective-permute-start(f32[96,384]{1,0:T(8,128)} %add.54.refs_2_), channel_id=1, source_target_pairs={{0,16},{16,32},{32,48},{48,0},{1,17},{17,33},{33,49},{49,1},{2,18}... | collective-permute-start | bytes 442376 | tf_op jit(solution)/shard_map/ppermute | solution.py:25
  69.2 10.8 %collective-permute-start.19 = (f32[96,384]{1,0:T(8,128)}, f32[96,384]{1,0:T(8,128)S(1)}, u32[]{:S(2)}, u32[]{:S(2)}) collective-permute-start(f32[96,384]{1,0:T(8,128)} %add.54.refs_2_), channel_id=1, source_target_pairs={{0,32},{16,48},{32,0},{48,16},{1,33},{17,49},{33,1},{49,17},{2,34}... | collective-permute-start | bytes 442376 | tf_op jit(solution)/shard_map/ppermute | solution.py:25
  73.0 7.0 %collective-permute-start.18 = (f32[96,384]{1,0:T(8,128)}, f32[96,384]{1,0:T(8,128)S(1)}, u32[]{:S(2)}, u32[]{:S(2)}) collective-permute-start(f32[96,384]{1,0:T(8,128)} %add.54.refs_2_), channel_id=1, source_target_pairs={{0,48},{16,0},{32,16},{48,32},{1,49},{17,1},{33,17},{49,33},{2,50}... | collective-permute-start | bytes 442376 | tf_op jit(solution)/shard_map/ppermute | solution.py:25
  74.2 13.8 %collective-permute-start.17 = (f32[2,96,192]{2,1,0:T(8,128)S(1)}, f32[2,96,192]{2,1,0:T(8,128)S(1)}, u32[]{:S(2)}, u32[]{:S(2)}) collective-permute-start(f32[2,96,192]{2,1,0:T(8,128)S(1)} %fusion.12), channel_id=1, source_target_pairs={{0,8},{8,0},{1,9},{9,1},{2,10},{10,2},{3,11},{11,3},{4,12},{12,4},... | collective-permute-start | bytes 442376 | tf_op jit(solution)/shard_map/ppermute | solution.py:25
  84.6 12.5 %collective-permute-start.22 = (f32[96,384]{1,0:T(8,128)S(1)}, f32[96,384]{1,0:T(8,128)S(1)}, u32[]{:S(2)}, u32[]{:S(2)}) collective-permute-start(f32[96,384]{1,0:T(8,128)S(1)} %get-tuple-element.63), channel_id=1, source_target_pairs={{0,128},{64,192},{128,0},{192,64},{1,129},{65,193},{129,1},{193,65... | collective-permute-start | bytes 442376 | tf_op jit(solution)/shard_map/ppermute | solution.py:25
  87.5 12.2 %collective-permute-start.23 = (f32[96,384]{1,0:T(8,128)S(1)}, f32[96,384]{1,0:T(8,128)S(1)}, u32[]{:S(2)}, u32[]{:S(2)}) collective-permute-start(f32[96,384]{1,0:T(8,128)S(1)} %get-tuple-element.64), channel_id=1, source_target_pairs={{0,192},{64,0},{128,64},{192,128},{1,193},{65,1},{129,65},{193,129... | collective-permute-start | bytes 442376 | tf_op jit(solution)/shard_map/ppermute | solution.py:25
  100.2 11.5 %collective-permute-start.25 = (f32[96,384]{1,0:T(8,128)S(1)}, f32[96,384]{1,0:T(8,128)S(1)}, u32[]{:S(2)}, u32[]{:S(2)}) collective-permute-start(f32[96,384]{1,0:T(8,128)S(1)} %get-tuple-element.81.refs_2_), channel_id=1, source_target_pairs={{0,128},{64,192},{128,0},{192,64},{1,129},{65,193},{129,1},{193,65... | collective-permute-start | bytes 442376 | tf_op jit(solution)/shard_map/ppermute | solution.py:25
  100.9 14.1 %collective-permute-start.24 = (f32[96,384]{1,0:T(8,128)S(1)}, f32[96,384]{1,0:T(8,128)S(1)}, u32[]{:S(2)}, u32[]{:S(2)}) collective-permute-start(f32[96,384]{1,0:T(8,128)S(1)} %get-tuple-element.81.refs_2_), channel_id=1, source_target_pairs={{0,192},{64,0},{128,64},{192,128},{1,193},{65,1},{129,65},{193,129... | collective-permute-start | bytes 442376 | tf_op jit(solution)/shard_map/ppermute | solution.py:25
  117.6 9.9 %collective-permute-start.28 = (f32[96,384]{1,0:T(8,128)S(1)}, f32[96,384]{1,0:T(8,128)S(1)}, u32[]{:S(2)}, u32[]{:S(2)}) collective-permute-start(f32[96,384]{1,0:T(8,128)S(1)} %get-tuple-element.67), channel_id=1, source_target_pairs={{0,32},{16,48},{32,0},{48,16},{1,33},{17,49},{33,1},{49,17},{2,34}... | collective-permute-start | bytes 442376 | tf_op jit(solution)/shard_map/ppermute | solution.py:25
  120.9 6.6 %collective-permute-start.29 = (f32[96,384]{1,0:T(8,128)S(1)}, f32[96,384]{1,0:T(8,128)S(1)}, u32[]{:S(2)}, u32[]{:S(2)}) collective-permute-start(f32[96,384]{1,0:T(8,128)S(1)} %get-tuple-element.68), channel_id=1, source_target_pairs={{0,48},{16,0},{32,16},{48,32},{1,49},{17,1},{33,17},{49,33},{2,50}... | collective-permute-start | bytes 442376 | tf_op jit(solution)/shard_map/ppermute | solution.py:25
  132.0 7.4 %collective-permute-start.34 = (f32[96,384]{1,0:T(8,128)S(1)}, f32[96,384]{1,0:T(8,128)S(1)}, u32[]{:S(2)}, u32[]{:S(2)}) collective-permute-start(f32[96,384]{1,0:T(8,128)S(1)} %get-tuple-element.76), channel_id=1, source_target_pairs={{0,1},{1,2},{2,3},{3,0},{4,5},{5,6},{6,7},{7,4},{8,9},{9,10},{10,1... | collective-permute-start | bytes 442376 | tf_op jit(solution)/shard_map/ppermute | solution.py:25
  132.2 9.2 %collective-permute-start.35 = (f32[96,384]{1,0:T(8,128)S(1)}, f32[96,384]{1,0:T(8,128)S(1)}, u32[]{:S(2)}, u32[]{:S(2)}) collective-permute-start(f32[96,384]{1,0:T(8,128)S(1)} %get-tuple-element.77), channel_id=1, source_target_pairs={{0,2},{1,3},{2,0},{3,1},{4,6},{5,7},{6,4},{7,5},{8,10},{9,11},{10,... | collective-permute-start | bytes 442376 | tf_op jit(solution)/shard_map/ppermute | solution.py:25
  134.6 7.9 %collective-permute-start.36 = (f32[96,384]{1,0:T(8,128)S(1)}, f32[96,384]{1,0:T(8,128)S(1)}, u32[]{:S(2)}, u32[]{:S(2)}) collective-permute-start(f32[96,384]{1,0:T(8,128)S(1)} %get-tuple-element.78), channel_id=1, source_target_pairs={{0,3},{1,0},{2,1},{3,2},{4,7},{5,4},{6,5},{7,6},{8,11},{9,8},{10,9... | collective-permute-start | bytes 442376 | tf_op jit(solution)/shard_map/ppermute | solution.py:25
  136.0 11.2 %collective-permute-start.38 = (f32[2,96,192]{2,1,0:T(8,128)S(1)}, f32[2,96,192]{2,1,0:T(8,128)S(1)}, u32[]{:S(2)}, u32[]{:S(2)}) collective-permute-start(f32[2,96,192]{2,1,0:T(8,128)S(1)} %fusion.14), channel_id=1, source_target_pairs={{0,8},{8,0},{1,9},{9,1},{2,10},{10,2},{3,11},{11,3},{4,12},{12,4},... | collective-permute-start | bytes 442376 | tf_op jit(solution)/shard_map/ppermute | solution.py:25
  139.1 9.9 %collective-permute-start.31 = (f32[96,384]{1,0:T(8,128)S(1)}, f32[96,384]{1,0:T(8,128)S(1)}, u32[]{:S(2)}, u32[]{:S(2)}) collective-permute-start(f32[96,384]{1,0:T(8,128)S(1)} %get-tuple-element.72), channel_id=1, source_target_pairs={{0,1},{1,2},{2,3},{3,0},{4,5},{5,6},{6,7},{7,4},{8,9},{9,10},{10,1... | collective-permute-start | bytes 442376 | tf_op jit(solution)/shard_map/ppermute | solution.py:25
  139.4 9.5 %collective-permute-start.32 = (f32[96,384]{1,0:T(8,128)S(1)}, f32[96,384]{1,0:T(8,128)S(1)}, u32[]{:S(2)}, u32[]{:S(2)}) collective-permute-start(f32[96,384]{1,0:T(8,128)S(1)} %get-tuple-element.73), channel_id=1, source_target_pairs={{0,2},{1,3},{2,0},{3,1},{4,6},{5,7},{6,4},{7,5},{8,10},{9,11},{10,... | collective-permute-start | bytes 442376 | tf_op jit(solution)/shard_map/ppermute | solution.py:25
  141.5 7.8 %collective-permute-start.33 = (f32[96,384]{1,0:T(8,128)S(1)}, f32[96,384]{1,0:T(8,128)S(1)}, u32[]{:S(2)}, u32[]{:S(2)}) collective-permute-start(f32[96,384]{1,0:T(8,128)S(1)} %get-tuple-element.74), channel_id=1, source_target_pairs={{0,3},{1,0},{2,1},{3,2},{4,7},{5,4},{6,5},{7,6},{8,11},{9,8},{10,9... | collective-permute-start | bytes 442376 | tf_op jit(solution)/shard_map/ppermute | solution.py:25
  142.5 12.4 %collective-permute-start.37 = (f32[96,384]{1,0:T(8,128)S(1)}, f32[96,384]{1,0:T(8,128)S(1)}, u32[]{:S(2)}, u32[]{:S(2)}) collective-permute-start(f32[96,384]{1,0:T(8,128)S(1)} %add_add_fusion), channel_id=1, source_target_pairs={{0,4},{4,0},{1,5},{5,1},{2,6},{6,2},{3,7},{7,3},{8,12},{12,8},{9,1... | collective-permute-start | bytes 442376 | tf_op jit(solution)/shard_map/ppermute | solution.py:25
  (22 other events, 166.4 us)

commit v3 on v2

--- a/solution.py
+++ b/solution.py
@@ -301,17 +301,20 @@
     )
     back = swapped(back[0] + sum(shift(back[d], "y", d) for d in (1, 2, 3)))
 
-    def summed(r):
-        values = call(
+    def terms_of(r):
+        return call(
             functools.partial(back_right_kernel, r),
             place,
             [back, *rights],
             [shape(rows, cols)] * 4,
         )
+
+    def summed(values):
         return values[0] + sum(shift(values[f], "x", f) for f in (1, 2, 3))
 
-    away = shift(summed(1), "zh", 1)
-    update = summed(0) + away
+    away, home = summed(terms_of(1)), list(terms_of(0))
+    home[3], away = lax.optimization_barrier((home[3], away))
+    update = summed(home) + shift(away, "zh", 1)
     return (update, *moments)
 
 

time: 157 us -> 159 us (1.013)
  starting transfers between devices: 69 us -> 70.9 us
    ppermute x39, starting transfers between devices: 60.8 us -> 62.7 us  [shift(): return lax.ppermute(value, axis, [(i, (i + by) % n) for i in range(n)])]
  transfers between devices with their start and end apart: 41 -> 41, of which waited for: 19 -> 18; matrix products, arithmetic and copies ran while one was open for 3% -> 2% of each run, Pallas kernels for 9% -> 9%
where the time goes in v3:
time: 159 us
  starting transfers between devices  70.9 us (45%)
  waiting for transfers between devices  56.5 us (36%)
  Pallas kernels  18.5 us (12%)
  local copies, waits for them, and re-layouts  6.15 us (4%)
  other arithmetic  5.48 us (3%)
    ppermute x39, starting transfers between devices, shift(): return lax.ppermute(value, axis, [(i, (i + by) % n) for i in range(n)])  62.7 us
    ppermute x39, waiting for transfers between devices, shift(): return lax.ppermute(value, axis, [(i, (i + by) % n) for i in range(n)])  55.9 us
    pallas_call x9, Pallas kernels, call(): pl.pallas_call(kernel, out_shape=outs, in_specs=[pl.BlockSpec(memory_spac...  18.5 us
    unnamed x26, local copies, waits for them, and re-layouts  4.18 us
    all_to_all x1, starting transfers between devices, body(): left = lax.all_to_all(packs, 'y', 0, 0, tiled=True)  4.18 us
    all_to_all x1, starting transfers between devices, copies_sent(): return lax.all_to_all(copies, axis, 0, 0, tiled=True)  4.01 us
  transfers between devices with their start and end apart: 41, of which 18 were waited for; matrix products, arithmetic and copies ran while one was open for 2% of the time, Pallas kernels for 9%

profile of v3, /device:TPU:33, one launch (start us, length us, event | category | flops | bytes accessed | tf_op | source)
XLA Modules:
  0.0 158.5 jit_solution(16026392018820874433)
XLA Ops:
  2.5 4.0 %all-to-all-start = ((f32[4,96,384]{2,1,0:T(8,128)}), f32[4,96,384]{2,1,0:T(8,128)S(1)}, u32[]{:S(2)}, u32[]{:S(2)}) async-start(f32[4,96,384]{2,1,0:T(8,128)} %broadcast_in_dim.2), calls=%async_computation | async-start | bytes 1179648 | tf_op jit(solution)/shard_map/all_to_all | solution.py:200
  9.1 2.8 %collective-permute-start.3 = (f32[96,384]{1,0:T(8,128)S(1)}, f32[96,384]{1,0:T(8,128)S(1)}, u32[]{:S(2)}, u32[]{:S(2)}) collective-permute-start(f32[96,384]{1,0:T(8,128)S(1)} %copy-done.12), channel_id=1, source_target_pairs={{0,128},{64,192},{128,0},{192,64},{1,129},{65,193},{129,1},{193,65... | collective-permute-start | bytes 442376 | tf_op jit(solution)/shard_map/ppermute | solution.py:25
  12.8 4.5 %collective-permute-start.1 = (f32[96,384]{1,0:T(8,128)S(1)}, f32[96,384]{1,0:T(8,128)S(1)}, u32[]{:S(2)}, u32[]{:S(2)}) collective-permute-start(f32[96,384]{1,0:T(8,128)S(1)} %shard_map.77), channel_id=1, source_target_pairs={{0,4},{4,0},{1,5},{5,1},{2,6},{6,2},{3,7},{7,3},{8,12},{12,8},{9,1... | collective-permute-start | bytes 442376 | tf_op jit(solution)/shard_map/ppermute | solution.py:25
  18.8 4.2 %all-to-all-start.1 = ((f32[4,96,384]{2,1,0:T(8,128)}), f32[4,96,384]{2,1,0:T(8,128)S(1)}, u32[]{:S(2)}, u32[]{:S(2)}) async-start(f32[4,96,384]{2,1,0:T(8,128)} %shard_map.76), calls=%async_computation.1 | async-start | bytes 1179648 | tf_op jit(solution)/shard_map/all_to_all | solution.py:246
  23.0 5.1 %collective-permute-done.3 = f32[96,384]{1,0:T(8,128)S(1)} collective-permute-done((f32[96,384]{1,0:T(8,128)S(1)}, f32[96,384]{1,0:T(8,128)S(1)}, u32[]{:S(2)}, u32[]{:S(2)}) %collective-permute-start.3) | collective-permute-done | bytes 147488 | tf_op jit(solution)/shard_map/ppermute | solution.py:25
  28.2 2.8 %collective-permute-start.11 = (f32[4,96,384]{2,1,0:T(8,128)S(1)}, f32[4,96,384]{2,1,0:T(8,128)S(1)}, u32[]{:S(2)}, u32[]{:S(2)}) collective-permute-start(f32[4,96,384]{2,1,0:T(8,128)S(1)} %pad_maximum_fusion.1.refs_5_), channel_id=1, source_target_pairs={{0,48},{16,0},{32,16},{48,32},{1,49},{17,1},{33,17},{49,33},{2,50}... | collective-permute-start | bytes 1769480 | tf_op jit(solution)/shard_map/ppermute | solution.py:25
  31.6 4.6 %collective-permute-start.5 = (f32[4,96,384]{2,1,0:T(8,128)S(1)}, f32[4,96,384]{2,1,0:T(8,128)S(1)}, u32[]{:S(2)}, u32[]{:S(2)}) collective-permute-start(f32[4,96,384]{2,1,0:T(8,128)S(1)} %all-to-all-done.1.refs_0_), channel_id=1, source_target_pairs={{0,4},{4,0},{1,5},{5,1},{2,6},{6,2},{3,7},{7,3},{8,12},{12,8},{9,1... | collective-permute-start | bytes 1769480 | tf_op jit(solution)/shard_map/ppermute | solution.py:25
  36.2 3.0 %collective-permute-start.7 = (f32[2,96,384]{2,1,0:T(8,128)S(1)}, f32[2,96,384]{2,1,0:T(8,128)S(1)}, u32[]{:S(2)}, u32[]{:S(2)}) collective-permute-start(f32[2,96,384]{2,1,0:T(8,128)S(1)} %pad_maximum_fusion.2.refs_0_), channel_id=1, source_target_pairs={{0,3},{1,0},{2,1},{3,2},{4,7},{5,4},{6,5},{7,6},{8,11},{9,8},{10,9... | collective-permute-start | bytes 884744 | tf_op jit(solution)/shard_map/ppermute | solution.py:25
  39.1 4.6 %collective-permute-done.11.refs_7_ = f32[4,96,384]{2,1,0:T(8,128)S(1)} collective-permute-done((f32[4,96,384]{2,1,0:T(8,128)S(1)}, f32[4,96,384]{2,1,0:T(8,128)S(1)}, u32[]{:S(2)}, u32[]{:S(2)}) %collective-permute-start.11) | collective-permute-done | bytes 589856 | tf_op jit(solution)/shard_map/ppermute | solution.py:25
  43.7 3.4 %collective-permute-start.13 = (f32[2,96,384]{2,1,0:T(8,128)S(1)}, f32[2,96,384]{2,1,0:T(8,128)S(1)}, u32[]{:S(2)}, u32[]{:S(2)}) collective-permute-start(f32[2,96,384]{2,1,0:T(8,128)S(1)} %slice.43), channel_id=1, source_target_pairs={{0,48},{16,0},{32,16},{48,32},{1,49},{17,1},{33,17},{49,33},{2,50}... | collective-permute-start | bytes 884744 | tf_op jit(solution)/shard_map/ppermute | solution.py:25
  47.3 3.0 %collective-permute-start.9 = (f32[1,96,384]{2,1,0:T(8,128)S(1)}, f32[1,96,384]{2,1,0:T(8,128)S(1)}, u32[]{:S(2)}, u32[]{:S(2)}) collective-permute-start(f32[1,96,384]{2,1,0:T(8,128)S(1)} %slice.41), channel_id=1, source_target_pairs={{0,3},{1,0},{2,1},{3,2},{4,7},{5,4},{6,5},{7,6},{8,11},{9,8},{10,9... | collective-permute-start | bytes 442376 | tf_op jit(solution)/shard_map/ppermute | solution.py:25
  52.4 3.7 %collective-permute-done.8.refs_3_ = f32[1,96,384]{2,1,0:T(8,128)S(1)} collective-permute-done((f32[1,96,384]{2,1,0:T(8,128)S(1)}, f32[1,96,384]{2,1,0:T(8,128)S(1)}, u32[]{:S(2)}, u32[]{:S(2)}) %collective-permute-start.8) | collective-permute-done | bytes 147488 | tf_op jit(solution)/shard_map/ppermute | solution.py:25
  60.3 2.5 %shard_map.78 = (f32[96,384]{1,0:T(8,128)S(1)}, f32[96,384]{1,0:T(8,128)S(1)}, f32[16,96,384]{2,1,0:T(8,128)S(1)}) custom-call(s32[5]{0:T(128)S(1)} %stack.74.place, f32[2,96,384]{2,1,0:T(8,128)S(1)} %copy-done.7, f32[2,96,384]{2,1,0:T(8,128)S(1)} %collective-permute-done.6.refs_1_, f32[2,96,384]{2,1,0:T(8,128)S(1)} %collective-permute-done.7.refs_2_, ...), custom_call_target="tpu_custom_call" | custom-call | tf_op jit(solution)/shard_map/pallas_call | solution.py:43
  62.8 2.8 %collective-permute-start.14 = (f32[96,384]{1,0:T(8,128)S(1)}, f32[96,384]{1,0:T(8,128)S(1)}, u32[]{:S(2)}, u32[]{:S(2)}) collective-permute-start(f32[96,384]{1,0:T(8,128)S(1)} %get-tuple-element.49), channel_id=1, source_target_pairs={{0,8},{8,0},{1,9},{9,1},{2,10},{10,2},{3,11},{11,3},{4,12},{12,4},... | collective-permute-start | bytes 442376 | tf_op jit(solution)/shard_map/ppermute | solution.py:25
  69.2 3.9 %collective-permute-start.19 = (f32[96,384]{1,0:T(8,128)}, f32[96,384]{1,0:T(8,128)S(1)}, u32[]{:S(2)}, u32[]{:S(2)}) collective-permute-start(f32[96,384]{1,0:T(8,128)} %add.54.refs_2_), channel_id=1, source_target_pairs={{0,32},{16,48},{32,0},{48,16},{1,33},{17,49},{33,1},{49,17},{2,34}... | collective-permute-start | bytes 442376 | tf_op jit(solution)/shard_map/ppermute | solution.py:25
  75.2 3.2 %shard_map.79 = (bf16[4,4,192,192]{3,2,1,0:T(8,128)(2,1)S(1)}, bf16[4,4,192,192]{3,2,1,0:T(8,128)(2,1)S(1)}, bf16[4,4,192,192]{3,2,1,0:T(8,128)(2,1)S(1)}, bf16[4,4,192,192]{3,2,1,0:T(8,128)(2,1)S(1)}) custom-call(s32[5]{0:T(128)S(1)} %stack.74.place, f32[4,96,384]{2,1,0:T(8,128)S(1)} %all-to-all-done.1.refs_0_, ...), custom_call_target="tpu_custom_call" | custom-call | tf_op jit(solution)/shard_map/pallas_call | solution.py:43
  80.0 2.1 %shard_map.81 = (f32[96,384]{1,0:T(8,128)S(1)}, f32[96,384]{1,0:T(8,128)S(1)}, f32[96,384]{1,0:T(8,128)S(1)}, f32[96,384]{1,0:T(8,128)S(1)}) custom-call(s32[5]{0:T(128)S(1)} %stack.74.place, bf16[4,4,192,192]{3,2,1,0:T(8,128)(2,1)S(1)} %get-tuple-element.53.refs_0_, bf16[4,4,192,192]{3,2,1,0:T(8,128)(2,1)S(1)} %get-tuple-element.54.refs_1_, ...), custom_call_target="tpu_custom_call" | custom-call | tf_op jit(solution)/shard_map/pallas_call | solution.py:43
  82.1 2.4 %collective-permute-start.21 = (f32[96,384]{1,0:T(8,128)S(1)}, f32[96,384]{1,0:T(8,128)S(1)}, u32[]{:S(2)}, u32[]{:S(2)}) collective-permute-start(f32[96,384]{1,0:T(8,128)S(1)} %get-tuple-element.64), channel_id=1, source_target_pairs={{0,64},{64,128},{128,192},{192,0},{1,65},{65,129},{129,193},{193,1... | collective-permute-start | bytes 442376 | tf_op jit(solution)/shard_map/ppermute | solution.py:25
  84.6 3.0 %collective-permute-start.22 = (f32[96,384]{1,0:T(8,128)S(1)}, f32[96,384]{1,0:T(8,128)S(1)}, u32[]{:S(2)}, u32[]{:S(2)}) collective-permute-start(f32[96,384]{1,0:T(8,128)S(1)} %get-tuple-element.65), channel_id=1, source_target_pairs={{0,128},{64,192},{128,0},{192,64},{1,129},{65,193},{129,1},{193,65... | collective-permute-start | bytes 442376 | tf_op jit(solution)/shard_map/ppermute | solution.py:25
  88.4 8.6 %collective-permute-done.22 = f32[96,384]{1,0:T(8,128)S(1)} collective-permute-done((f32[96,384]{1,0:T(8,128)S(1)}, f32[96,384]{1,0:T(8,128)S(1)}, u32[]{:S(2)}, u32[]{:S(2)}) %collective-permute-start.22) | collective-permute-done | bytes 147488 | tf_op jit(solution)/shard_map/ppermute | solution.py:25
  97.1 2.7 %collective-permute-done.23 = f32[96,384]{1,0:T(8,128)S(1)} collective-permute-done((f32[96,384]{1,0:T(8,128)S(1)}, f32[96,384]{1,0:T(8,128)S(1)}, u32[]{:S(2)}, u32[]{:S(2)}) %collective-permute-start.23) | collective-permute-done | bytes 147488 | tf_op jit(solution)/shard_map/ppermute | solution.py:25
  102.0 2.7 %shard_map.80 = (bf16[8,384,384]{2,1,0:T(8,128)(2,1)S(1)}, bf16[8,384,384]{2,1,0:T(8,128)(2,1)S(1)}) custom-call(s32[5]{0:T(128)S(1)} %stack.74.place, f32[16,96,384]{2,1,0:T(8,128)S(1)} %get-tuple-element.55.own, f32[16,96,384]{2,1,0:T(8,128)} %collective-permute-done.16.away), custom_call_target="tpu_custom_call" | custom-call | tf_op jit(solution)/shard_map/pallas_call | solution.py:43
  104.7 6.9 %collective-permute-done.25.refs_4_ = f32[96,384]{1,0:T(8,128)S(1)} collective-permute-done((f32[96,384]{1,0:T(8,128)S(1)}, f32[96,384]{1,0:T(8,128)S(1)}, u32[]{:S(2)}, u32[]{:S(2)}) %collective-permute-start.25) | collective-permute-done | bytes 147488 | tf_op jit(solution)/shard_map/ppermute | solution.py:25
  111.6 3.3 %collective-permute-done.24.refs_3_ = f32[96,384]{1,0:T(8,128)S(1)} collective-permute-done((f32[96,384]{1,0:T(8,128)S(1)}, f32[96,384]{1,0:T(8,128)S(1)}, u32[]{:S(2)}, u32[]{:S(2)}) %collective-permute-start.24) | collective-permute-done | bytes 147488 | tf_op jit(solution)/shard_map/ppermute | solution.py:25
  115.0 2.1 %shard_map.82 = (f32[96,384]{1,0:T(8,128)S(1)}, f32[96,384]{1,0:T(8,128)S(1)}, f32[96,384]{1,0:T(8,128)S(1)}, f32[96,384]{1,0:T(8,128)S(1)}) custom-call(s32[5]{0:T(128)S(1)} %stack.74.place, bf16[4,4,192,192]{3,2,1,0:T(8,128)(2,1)S(1)} %get-tuple-element.58.refs_0_, bf16[4,4,192,192]{3,2,1,0:T(8,128)(2,1)S(1)} %get-tuple-element.59.refs_1_, ...), custom_call_target="tpu_custom_call" | custom-call | tf_op jit(solution)/shard_map/pallas_call | solution.py:43
  117.6 3.2 %collective-permute-start.28 = (f32[96,384]{1,0:T(8,128)S(1)}, f32[96,384]{1,0:T(8,128)S(1)}, u32[]{:S(2)}, u32[]{:S(2)}) collective-permute-start(f32[96,384]{1,0:T(8,128)S(1)} %get-tuple-element.69), channel_id=1, source_target_pairs={{0,32},{16,48},{32,0},{48,16},{1,33},{17,49},{33,1},{49,17},{2,34}... | collective-permute-start | bytes 442376 | tf_op jit(solution)/shard_map/ppermute | solution.py:25
  120.9 2.3 %collective-permute-done.27 = f32[96,384]{1,0:T(8,128)S(1)} collective-permute-done((f32[96,384]{1,0:T(8,128)S(1)}, f32[96,384]{1,0:T(8,128)S(1)}, u32[]{:S(2)}, u32[]{:S(2)}) %collective-permute-start.27) | collective-permute-done | bytes 147488 | tf_op jit(solution)/shard_map/ppermute | solution.py:25
  123.2 4.3 %collective-permute-done.28 = f32[96,384]{1,0:T(8,128)S(1)} collective-permute-done((f32[96,384]{1,0:T(8,128)S(1)}, f32[96,384]{1,0:T(8,128)S(1)}, u32[]{:S(2)}, u32[]{:S(2)}) %collective-permute-start.28) | collective-permute-done | bytes 147488 | tf_op jit(solution)/shard_map/ppermute | solution.py:25
  132.2 2.4 %collective-permute-start.34 = (f32[96,384]{1,0:T(8,128)S(1)}, f32[96,384]{1,0:T(8,128)S(1)}, u32[]{:S(2)}, u32[]{:S(2)}) collective-permute-start(f32[96,384]{1,0:T(8,128)S(1)} %get-tuple-element.79), channel_id=1, source_target_pairs={{0,2},{1,3},{2,0},{3,1},{4,6},{5,7},{6,4},{7,5},{8,10},{9,11},{10,... | collective-permute-start | bytes 442376 | tf_op jit(solution)/shard_map/ppermute | solution.py:25
  141.8 3.5 %collective-permute-start.36 = (f32[96,384]{1,0:T(8,128)S(1)}, f32[96,384]{1,0:T(8,128)S(1)}, u32[]{:S(2)}, u32[]{:S(2)}) collective-permute-start(f32[96,384]{1,0:T(8,128)S(1)} %get-tuple-element.81), channel_id=1, source_target_pairs={{0,3},{1,0},{2,1},{3,2},{4,7},{5,4},{6,5},{7,6},{8,11},{9,8},{10,9... | collective-permute-start | bytes 442376 | tf_op jit(solution)/shard_map/ppermute | solution.py:25
  145.3 4.1 %collective-permute-start.37 = (f32[96,384]{1,0:T(8,128)S(1)}, f32[96,384]{1,0:T(8,128)S(1)}, u32[]{:S(2)}, u32[]{:S(2)}) collective-permute-start(f32[96,384]{1,0:T(8,128)S(1)} %add_add_fusion.1), channel_id=1, source_target_pairs={{0,4},{4,0},{1,5},{5,1},{2,6},{6,2},{3,7},{7,3},{8,12},{12,8},{9,1... | collective-permute-start | bytes 442376 | tf_op jit(solution)/shard_map/ppermute | solution.py:25
  150.4 7.5 %collective-permute-done.37 = f32[96,384]{1,0:T(8,128)S(1)} collective-permute-done((f32[96,384]{1,0:T(8,128)S(1)}, f32[96,384]{1,0:T(8,128)S(1)}, u32[]{:S(2)}, u32[]{:S(2)}) %collective-permute-start.37) | collective-permute-done | bytes 147488 | tf_op jit(solution)/shard_map/ppermute | solution.py:25
  (108 shorter events, 38.4 us)
Async XLA Ops:
  2.5 14.8 %all-to-all-start = ((f32[4,96,384]{2,1,0:T(8,128)}), f32[4,96,384]{2,1,0:T(8,128)S(1)}, u32[]{:S(2)}, u32[]{:S(2)}) async-start(f32[4,96,384]{2,1,0:T(8,128)} %broadcast_in_dim.2), calls=%async_computation | async-start | bytes 1179648 | tf_op jit(solution)/shard_map/all_to_all | solution.py:200
  7.4 15.5 %collective-permute-start.2 = (f32[96,384]{1,0:T(8,128)S(1)}, f32[96,384]{1,0:T(8,128)S(1)}, u32[]{:S(2)}, u32[]{:S(2)}) collective-permute-start(f32[96,384]{1,0:T(8,128)S(1)} %copy-done.12), channel_id=1, source_target_pairs={{0,64},{64,128},{128,192},{192,0},{1,65},{65,129},{129,193},{193,1... | collective-permute-start | bytes 442376 | tf_op jit(solution)/shard_map/ppermute | solution.py:25
  9.1 13.9 %collective-permute-start.4 = (f32[96,384]{1,0:T(8,128)S(1)}, f32[96,384]{1,0:T(8,128)S(1)}, u32[]{:S(2)}, u32[]{:S(2)}) collective-permute-start(f32[96,384]{1,0:T(8,128)S(1)} %copy-done.12), channel_id=1, source_target_pairs={{0,192},{64,0},{128,64},{192,128},{1,193},{65,1},{129,65},{193,129... | collective-permute-start | bytes 442376 | tf_op jit(solution)/shard_map/ppermute | solution.py:25
  9.1 19.0 %collective-permute-start.3 = (f32[96,384]{1,0:T(8,128)S(1)}, f32[96,384]{1,0:T(8,128)S(1)}, u32[]{:S(2)}, u32[]{:S(2)}) collective-permute-start(f32[96,384]{1,0:T(8,128)S(1)} %copy-done.12), channel_id=1, source_target_pairs={{0,128},{64,192},{128,0},{192,64},{1,129},{65,193},{129,1},{193,65... | collective-permute-start | bytes 442376 | tf_op jit(solution)/shard_map/ppermute | solution.py:25
  12.8 15.4 %collective-permute-start.1 = (f32[96,384]{1,0:T(8,128)S(1)}, f32[96,384]{1,0:T(8,128)S(1)}, u32[]{:S(2)}, u32[]{:S(2)}) collective-permute-start(f32[96,384]{1,0:T(8,128)S(1)} %shard_map.77), channel_id=1, source_target_pairs={{0,4},{4,0},{1,5},{5,1},{2,6},{6,2},{3,7},{7,3},{8,12},{12,8},{9,1... | collective-permute-start | bytes 442376 | tf_op jit(solution)/shard_map/ppermute | solution.py:25
  18.8 12.8 %all-to-all-start.1 = ((f32[4,96,384]{2,1,0:T(8,128)}), f32[4,96,384]{2,1,0:T(8,128)S(1)}, u32[]{:S(2)}, u32[]{:S(2)}) async-start(f32[4,96,384]{2,1,0:T(8,128)} %shard_map.76), calls=%async_computation.1 | async-start | bytes 1179648 | tf_op jit(solution)/shard_map/all_to_all | solution.py:246
  28.2 15.5 %collective-permute-start.11 = (f32[4,96,384]{2,1,0:T(8,128)S(1)}, f32[4,96,384]{2,1,0:T(8,128)S(1)}, u32[]{:S(2)}, u32[]{:S(2)}) collective-permute-start(f32[4,96,384]{2,1,0:T(8,128)S(1)} %pad_maximum_fusion.1.refs_5_), channel_id=1, source_target_pairs={{0,48},{16,0},{32,16},{48,32},{1,49},{17,1},{33,17},{49,33},{2,50}... | collective-permute-start | bytes 1769480 | tf_op jit(solution)/shard_map/ppermute | solution.py:25
  31.0 16.1 %collective-permute-start.10 = (f32[4,96,384]{2,1,0:T(8,128)S(1)}, f32[4,96,384]{2,1,0:T(8,128)S(1)}, u32[]{:S(2)}, u32[]{:S(2)}) collective-permute-start(f32[4,96,384]{2,1,0:T(8,128)S(1)} %pad_maximum_fusion.1.refs_5_), channel_id=1, source_target_pairs={{0,16},{16,32},{32,48},{48,0},{1,17},{17,33},{33,49},{49,1},{2,18}... | collective-permute-start | bytes 1769480 | tf_op jit(solution)/shard_map/ppermute | solution.py:25
  31.6 31.2 %collective-permute-start.5 = (f32[4,96,384]{2,1,0:T(8,128)S(1)}, f32[4,96,384]{2,1,0:T(8,128)S(1)}, u32[]{:S(2)}, u32[]{:S(2)}) collective-permute-start(f32[4,96,384]{2,1,0:T(8,128)S(1)} %all-to-all-done.1.refs_0_), channel_id=1, source_target_pairs={{0,4},{4,0},{1,5},{5,1},{2,6},{6,2},{3,7},{7,3},{8,12},{12,8},{9,1... | collective-permute-start | bytes 1769480 | tf_op jit(solution)/shard_map/ppermute | solution.py:25
  36.2 11.1 %collective-permute-start.7 = (f32[2,96,384]{2,1,0:T(8,128)S(1)}, f32[2,96,384]{2,1,0:T(8,128)S(1)}, u32[]{:S(2)}, u32[]{:S(2)}) collective-permute-start(f32[2,96,384]{2,1,0:T(8,128)S(1)} %pad_maximum_fusion.2.refs_0_), channel_id=1, source_target_pairs={{0,3},{1,0},{2,1},{3,2},{4,7},{5,4},{6,5},{7,6},{8,11},{9,8},{10,9... | collective-permute-start | bytes 884744 | tf_op jit(solution)/shard_map/ppermute | solution.py:25
  39.1 11.2 %collective-permute-start.6 = (f32[2,96,384]{2,1,0:T(8,128)S(1)}, f32[2,96,384]{2,1,0:T(8,128)S(1)}, u32[]{:S(2)}, u32[]{:S(2)}) collective-permute-start(f32[2,96,384]{2,1,0:T(8,128)S(1)} %pad_maximum_fusion.2.refs_0_), channel_id=1, source_target_pairs={{0,1},{1,2},{2,3},{3,0},{4,5},{5,6},{6,7},{7,4},{8,9},{9,10},{10,1... | collective-permute-start | bytes 884744 | tf_op jit(solution)/shard_map/ppermute | solution.py:25
  43.7 12.4 %collective-permute-start.13 = (f32[2,96,384]{2,1,0:T(8,128)S(1)}, f32[2,96,384]{2,1,0:T(8,128)S(1)}, u32[]{:S(2)}, u32[]{:S(2)}) collective-permute-start(f32[2,96,384]{2,1,0:T(8,128)S(1)} %slice.43), channel_id=1, source_target_pairs={{0,48},{16,0},{32,16},{48,32},{1,49},{17,1},{33,17},{49,33},{2,50}... | collective-permute-start | bytes 884744 | tf_op jit(solution)/shard_map/ppermute | solution.py:25
  47.2 9.0 %collective-permute-start.12 = (f32[2,96,384]{2,1,0:T(8,128)S(1)}, f32[2,96,384]{2,1,0:T(8,128)S(1)}, u32[]{:S(2)}, u32[]{:S(2)}) collective-permute-start(f32[2,96,384]{2,1,0:T(8,128)S(1)} %slice.42), channel_id=1, source_target_pairs={{0,16},{16,32},{32,48},{48,0},{1,17},{17,33},{33,49},{49,1},{2,18}... | collective-permute-start | bytes 884744 | tf_op jit(solution)/shard_map/ppermute | solution.py:25
  67.3 34.7 %collective-permute-start.16 = (f32[16,96,384]{2,1,0:T(8,128)S(1)}, f32[16,96,384]{2,1,0:T(8,128)}, u32[]{:S(2)}, u32[]{:S(2)}) collective-permute-start(f32[16,96,384]{2,1,0:T(8,128)S(1)} %get-tuple-element.55.own), channel_id=1, source_target_pairs={{0,8},{8,0},{1,9},{9,1},{2,10},{10,2},{3,11},{11,3},{4,12},{12,4},... | collective-permute-start | bytes 7077896 | tf_op jit(solution)/shard_map/ppermute | solution.py:25
  68.9 9.5 %collective-permute-start.20 = (f32[96,384]{1,0:T(8,128)}, f32[96,384]{1,0:T(8,128)S(1)}, u32[]{:S(2)}, u32[]{:S(2)}) collective-permute-start(f32[96,384]{1,0:T(8,128)} %add.54.refs_2_), channel_id=1, source_target_pairs={{0,16},{16,32},{32,48},{48,0},{1,17},{17,33},{33,49},{49,1},{2,18}... | collective-permute-start | bytes 442376 | tf_op jit(solution)/shard_map/ppermute | solution.py:25
  69.2 10.8 %collective-permute-start.19 = (f32[96,384]{1,0:T(8,128)}, f32[96,384]{1,0:T(8,128)S(1)}, u32[]{:S(2)}, u32[]{:S(2)}) collective-permute-start(f32[96,384]{1,0:T(8,128)} %add.54.refs_2_), channel_id=1, source_target_pairs={{0,32},{16,48},{32,0},{48,16},{1,33},{17,49},{33,1},{49,17},{2,34}... | collective-permute-start | bytes 442376 | tf_op jit(solution)/shard_map/ppermute | solution.py:25
  73.0 7.0 %collective-permute-start.18 = (f32[96,384]{1,0:T(8,128)}, f32[96,384]{1,0:T(8,128)S(1)}, u32[]{:S(2)}, u32[]{:S(2)}) collective-permute-start(f32[96,384]{1,0:T(8,128)} %add.54.refs_2_), channel_id=1, source_target_pairs={{0,48},{16,0},{32,16},{48,32},{1,49},{17,1},{33,17},{49,33},{2,50}... | collective-permute-start | bytes 442376 | tf_op jit(solution)/shard_map/ppermute | solution.py:25
  74.2 13.8 %collective-permute-start.17 = (f32[2,96,192]{2,1,0:T(8,128)S(1)}, f32[2,96,192]{2,1,0:T(8,128)S(1)}, u32[]{:S(2)}, u32[]{:S(2)}) collective-permute-start(f32[2,96,192]{2,1,0:T(8,128)S(1)} %fusion.12), channel_id=1, source_target_pairs={{0,8},{8,0},{1,9},{9,1},{2,10},{10,2},{3,11},{11,3},{4,12},{12,4},... | collective-permute-start | bytes 442376 | tf_op jit(solution)/shard_map/ppermute | solution.py:25
  84.6 12.5 %collective-permute-start.22 = (f32[96,384]{1,0:T(8,128)S(1)}, f32[96,384]{1,0:T(8,128)S(1)}, u32[]{:S(2)}, u32[]{:S(2)}) collective-permute-start(f32[96,384]{1,0:T(8,128)S(1)} %get-tuple-element.65), channel_id=1, source_target_pairs={{0,128},{64,192},{128,0},{192,64},{1,129},{65,193},{129,1},{193,65... | collective-permute-start | bytes 442376 | tf_op jit(solution)/shard_map/ppermute | solution.py:25
  87.5 12.2 %collective-permute-start.23 = (f32[96,384]{1,0:T(8,128)S(1)}, f32[96,384]{1,0:T(8,128)S(1)}, u32[]{:S(2)}, u32[]{:S(2)}) collective-permute-start(f32[96,384]{1,0:T(8,128)S(1)} %get-tuple-element.66), channel_id=1, source_target_pairs={{0,192},{64,0},{128,64},{192,128},{1,193},{65,1},{129,65},{193,129... | collective-permute-start | bytes 442376 | tf_op jit(solution)/shard_map/ppermute | solution.py:25
  100.2 11.5 %collective-permute-start.25 = (f32[96,384]{1,0:T(8,128)S(1)}, f32[96,384]{1,0:T(8,128)S(1)}, u32[]{:S(2)}, u32[]{:S(2)}) collective-permute-start(f32[96,384]{1,0:T(8,128)S(1)} %get-tuple-element.85.refs_2_), channel_id=1, source_target_pairs={{0,128},{64,192},{128,0},{192,64},{1,129},{65,193},{129,1},{193,65... | collective-permute-start | bytes 442376 | tf_op jit(solution)/shard_map/ppermute | solution.py:25
  100.9 14.1 %collective-permute-start.24 = (f32[96,384]{1,0:T(8,128)S(1)}, f32[96,384]{1,0:T(8,128)S(1)}, u32[]{:S(2)}, u32[]{:S(2)}) collective-permute-start(f32[96,384]{1,0:T(8,128)S(1)} %get-tuple-element.85.refs_2_), channel_id=1, source_target_pairs={{0,192},{64,0},{128,64},{192,128},{1,193},{65,1},{129,65},{193,129... | collective-permute-start | bytes 442376 | tf_op jit(solution)/shard_map/ppermute | solution.py:25
  117.6 9.9 %collective-permute-start.28 = (f32[96,384]{1,0:T(8,128)S(1)}, f32[96,384]{1,0:T(8,128)S(1)}, u32[]{:S(2)}, u32[]{:S(2)}) collective-permute-start(f32[96,384]{1,0:T(8,128)S(1)} %get-tuple-element.69), channel_id=1, source_target_pairs={{0,32},{16,48},{32,0},{48,16},{1,33},{17,49},{33,1},{49,17},{2,34}... | collective-permute-start | bytes 442376 | tf_op jit(solution)/shard_map/ppermute | solution.py:25
  120.9 6.6 %collective-permute-start.29 = (f32[96,384]{1,0:T(8,128)S(1)}, f32[96,384]{1,0:T(8,128)S(1)}, u32[]{:S(2)}, u32[]{:S(2)}) collective-permute-start(f32[96,384]{1,0:T(8,128)S(1)} %get-tuple-element.70), channel_id=1, source_target_pairs={{0,48},{16,0},{32,16},{48,32},{1,49},{17,1},{33,17},{49,33},{2,50}... | collective-permute-start | bytes 442376 | tf_op jit(solution)/shard_map/ppermute | solution.py:25
  132.0 7.4 %collective-permute-start.33 = (f32[96,384]{1,0:T(8,128)S(1)}, f32[96,384]{1,0:T(8,128)S(1)}, u32[]{:S(2)}, u32[]{:S(2)}) collective-permute-start(f32[96,384]{1,0:T(8,128)S(1)} %get-tuple-element.78), channel_id=1, source_target_pairs={{0,1},{1,2},{2,3},{3,0},{4,5},{5,6},{6,7},{7,4},{8,9},{9,10},{10,1... | collective-permute-start | bytes 442376 | tf_op jit(solution)/shard_map/ppermute | solution.py:25
  132.2 9.2 %collective-permute-start.34 = (f32[96,384]{1,0:T(8,128)S(1)}, f32[96,384]{1,0:T(8,128)S(1)}, u32[]{:S(2)}, u32[]{:S(2)}) collective-permute-start(f32[96,384]{1,0:T(8,128)S(1)} %get-tuple-element.79), channel_id=1, source_target_pairs={{0,2},{1,3},{2,0},{3,1},{4,6},{5,7},{6,4},{7,5},{8,10},{9,11},{10,... | collective-permute-start | bytes 442376 | tf_op jit(solution)/shard_map/ppermute | solution.py:25
  134.6 7.1 %collective-permute-start.35 = (f32[96,384]{1,0:T(8,128)S(1)}, f32[96,384]{1,0:T(8,128)S(1)}, u32[]{:S(2)}, u32[]{:S(2)}) collective-permute-start(f32[96,384]{1,0:T(8,128)S(1)} %get-tuple-element.80), channel_id=1, source_target_pairs={{0,3},{1,0},{2,1},{3,2},{4,7},{5,4},{6,5},{7,6},{8,11},{9,8},{10,9... | collective-permute-start | bytes 442376 | tf_op jit(solution)/shard_map/ppermute | solution.py:25
  136.0 13.4 %collective-permute-start.38 = (f32[2,96,192]{2,1,0:T(8,128)S(1)}, f32[2,96,192]{2,1,0:T(8,128)S(1)}, u32[]{:S(2)}, u32[]{:S(2)}) collective-permute-start(f32[2,96,192]{2,1,0:T(8,128)S(1)} %fusion.14), channel_id=1, source_target_pairs={{0,8},{8,0},{1,9},{9,1},{2,10},{10,2},{3,11},{11,3},{4,12},{12,4},... | collective-permute-start | bytes 442376 | tf_op jit(solution)/shard_map/ppermute | solution.py:25
  139.1 11.3 %collective-permute-start.31 = (f32[96,384]{1,0:T(8,128)S(1)}, f32[96,384]{1,0:T(8,128)S(1)}, u32[]{:S(2)}, u32[]{:S(2)}) collective-permute-start(f32[96,384]{1,0:T(8,128)S(1)} %get-tuple-element.74), channel_id=1, source_target_pairs={{0,1},{1,2},{2,3},{3,0},{4,5},{5,6},{6,7},{7,4},{8,9},{9,10},{10,1... | collective-permute-start | bytes 442376 | tf_op jit(solution)/shard_map/ppermute | solution.py:25
  139.4 10.9 %collective-permute-start.32 = (f32[96,384]{1,0:T(8,128)S(1)}, f32[96,384]{1,0:T(8,128)S(1)}, u32[]{:S(2)}, u32[]{:S(2)}) collective-permute-start(f32[96,384]{1,0:T(8,128)S(1)} %get-tuple-element.75), channel_id=1, source_target_pairs={{0,2},{1,3},{2,0},{3,1},{4,6},{5,7},{6,4},{7,5},{8,10},{9,11},{10,... | collective-permute-start | bytes 442376 | tf_op jit(solution)/shard_map/ppermute | solution.py:25
  141.8 8.5 %collective-permute-start.36 = (f32[96,384]{1,0:T(8,128)S(1)}, f32[96,384]{1,0:T(8,128)S(1)}, u32[]{:S(2)}, u32[]{:S(2)}) collective-permute-start(f32[96,384]{1,0:T(8,128)S(1)} %get-tuple-element.81), channel_id=1, source_target_pairs={{0,3},{1,0},{2,1},{3,2},{4,7},{5,4},{6,5},{7,6},{8,11},{9,8},{10,9... | collective-permute-start | bytes 442376 | tf_op jit(solution)/shard_map/ppermute | solution.py:25
  145.3 12.5 %collective-permute-start.37 = (f32[96,384]{1,0:T(8,128)S(1)}, f32[96,384]{1,0:T(8,128)S(1)}, u32[]{:S(2)}, u32[]{:S(2)}) collective-permute-start(f32[96,384]{1,0:T(8,128)S(1)} %add_add_fusion.1), channel_id=1, source_target_pairs={{0,4},{4,0},{1,5},{5,1},{2,6},{6,2},{3,7},{7,3},{8,12},{12,8},{9,1... | collective-permute-start | bytes 442376 | tf_op jit(solution)/shard_map/ppermute | solution.py:25
  (22 other events, 166.4 us)
